TPU v7x, 128 devices: a whole 4x4x4 slice. The times are simulated.
128 devices in a mesh: rows: 32 (over y, x, core), cls: 4 (over z).
Axes of the slice: x: 4, y: 4, z: 4, core: 2. Of those that a mesh axis runs over, the one named last changes fastest.
Arguments:
- data: bfloat16 [65536, 512], P('rows'), may hold values from -4 to 4
- projections: bfloat16 [512, 1536], replicated, may hold values from -1 to 1
- phases: float32 [1536], replicated, may hold values from -4 to 4
- targets: bfloat16 [65536, 1024], P('rows', 'cls'), may hold values from -8 to 8
- bounds: float32 [3, 2], replicated, may hold values from 0 to 4, as said below
- order: int32 [3], replicated, may hold values from 0 to 2, each once
Outputs:
- weights: float32 [3, 512, 1024], P(None, 'rows', 'cls')
- residual: float32 [65536, 1024], P('rows', 'cls')
Inputs may be any that keep to these rules, and one draw needn't show every extreme that they name: bounds[j, 1] is at least the largest eigenvalue of block j's gram, and bounds[j, 1] > bounds[j, 0] > 0. order names each block index once.
All inputs are finite; a program needn't handle non-finite values.
Results may differ from a plain program's by a relative error of at most 0.0014.
Values may be sent and summed in bfloat16 or wider, within the bound.
A program may use at most 64 MiB of HBM per device.

v0:
```python
import math

import jax
import jax.numpy as jnp
from jax import lax
from jax.sharding import PartitionSpec as P

F = 512
NBLK = 3
ITERS = 16


def cosine_features(data, projections, phases, offset, count):
    columns = lax.dynamic_slice_in_dim(projections, offset, count, 1)
    shifts = lax.dynamic_slice_in_dim(phases, offset, count, 0)
    angles = jnp.dot(data, columns, preferred_element_type=jnp.float32) + shifts[None, :]
    return (math.sqrt(2.0 / F) * jnp.cos(angles)).astype(jnp.bfloat16)


def chebyshev(apply_gram, moment, lower, upper):
    center = 0.5 * (upper + lower)
    half = 0.5 * (upper - lower)
    sigma = center / half
    direction = moment / center

    def advance(index, carry):
        solution, remain, direction, ratio_old = carry
        remain = remain - apply_gram(direction)
        ratio_new = 1.0 / (2.0 * sigma - ratio_old)
        direction = ratio_new * ratio_old * direction + 2.0 * ratio_new / half * remain
        return (solution + direction, remain, direction, ratio_new)

    final = lax.fori_loop(0, ITERS - 1, advance, (direction, moment, direction, 1.0 / sigma))
    return final[0]


def contract_rows(left, right):
    return lax.dot_general(
        left, right, (((0,), (0,)), ((), ())), preferred_element_type=jnp.float32
    )


def body(data, projections, phases, targets, bounds, order):
    rows_local = data.shape[0]
    classes_local = targets.shape[1]
    total_rows = rows_local * lax.axis_size("rows")
    slab = F // lax.axis_size("rows")
    slab_start = lax.axis_index("rows") * slab
    residual = targets.astype(jnp.float32)
    weights = jnp.zeros((NBLK, slab, classes_local), jnp.float32)
    for turn in range(NBLK):
        block = order[turn]
        features = cosine_features(data, projections, phases, block * F, F)
        residual_half = residual.astype(jnp.bfloat16)
        gram_part = contract_rows(features, features)
        moment_part = contract_rows(features, residual_half)
        lower = bounds[block, 0]
        upper = bounds[block, 1]
        gram_sum, moment_sum = lax.psum((gram_part, moment_part), "rows")
        moment = moment_sum / total_rows
        gram = gram_sum / total_rows + lower * jnp.eye(F, dtype=jnp.float32)

        def apply_whole(direction):
            return jnp.dot(
                gram, direction, precision=lax.Precision.HIGHEST, preferred_element_type=jnp.float32
            )

        solution = chebyshev(apply_whole, moment, lower, upper)
        own_rows = lax.dynamic_slice_in_dim(solution, slab_start, slab, 0)
        solution_half = solution.astype(jnp.bfloat16)
        weights = lax.dynamic_update_slice(
            weights, own_rows[None], (block, jnp.int32(0), jnp.int32(0))
        )
        residual = residual - jnp.dot(features, solution_half, preferred_element_type=jnp.float32)
    return (weights, residual)


def solution(mesh):
    return jax.shard_map(
        body,
        mesh=mesh,
        in_specs=(P("rows", None), P(), P(), P("rows", "cls"), P(), P()),
        out_specs=(P(None, "rows", "cls"), P("rows", "cls")),
        check_vma=False,
    )
```

profile of v0, /device:TPU:1, one launch (start us, length us, event | category | flops | bytes accessed | tf_op | source)
XLA Modules:
  0.0 604.2 jit_solution(6906739693880436029)
XLA Ops:
  11.4 16.5 %multiply_convert_fusion.2 = bf16[512,2048]{1,0:T(8,128)(2,1)S(1)} fusion(bf16[2048,512]{1,0:T(8,128)(2,1)S(1)} %copy-done, f32[512]{0:T(512)S(1)} %get-tuple-element.357, bf16[512,1536]{1,0:T(8,128)(2,1)} %param.13, s32[]{:T(128)S(6)} %select_n.14), kind=kOutput, calls=%fused_computation.8 | convolution fusion | flops 1076887552 | bytes 4720644 | tf_op jit(solution)/shard_map/dot_general | solution.py:16
  40.9 16.5 %multiply_convert_fusion.1 = bf16[512,2048]{1,0:T(8,128)(2,1)S(1)} fusion(bf16[2048,512]{1,0:T(8,128)(2,1)S(1)} %copy-done, f32[512]{0:T(512)S(1)} %get-tuple-element.358, bf16[512,1536]{1,0:T(8,128)(2,1)} %param.13, s32[]{:T(128)S(6)} %select_n.17), kind=kOutput, calls=%fused_computation.7 | convolution fusion | flops 1076887552 | bytes 4720644 | tf_op jit(solution)/shard_map/dot_general | solution.py:16
  61.0 80.3 %all-reduce.11.cloned.1.call-done = (f32[512,256]{1,0:T(8,128)}, f32[512,512]{1,0:T(8,128)}) async-done(((f32[512,256]{1,0:T(8,128)}, f32[512,512]{1,0:T(8,128)}), (f32[512,256]{1,0:T(8,128)}, f32[512,512]{1,0:T(8,128)})) %all-reduce.11.cloned.1.call-update) | async-done | bytes 1572880 | tf_op jit(solution)/shard_map/psum | solution.py:59
  145.8 70.2 %while.54 = (s32[]{:T(128)}, f32[512,256]{1,0:T(8,128)S(1)}, f32[512,256]{1,0:T(8,128)}, f32[512,256]{1,0:T(8,128)}, f32[]{:T(128)}, /*index=5*/f32[]{:T(128)}, ...) while((s32[]{:T(128)}, f32[512,256]{1,0:T(8,128)S(1)}, f32[512,256]{1,0:T(8,128)}, ...), condition=%wide.region_3.0_spmd, body=%wide.region_2.0_spmd.sunk | while | flops 805961728 | bytes 5243065 | solution.py:33
  224.7 16.5 %multiply_convert_fusion = bf16[512,2048]{1,0:T(8,128)(2,1)S(1)} fusion(bf16[2048,512]{1,0:T(8,128)(2,1)S(1)} %copy-done, f32[512]{0:T(512)S(1)} %get-tuple-element.356, bf16[512,1536]{1,0:T(8,128)(2,1)} %param.13, s32[]{:T(128)S(6)} %select_n.37), kind=kOutput, calls=%fused_computation.6 | convolution fusion | flops 1076887552 | bytes 4720644 | tf_op jit(solution)/shard_map/dot_general | solution.py:16
  244.8 83.0 %all-reduce.9.cloned.1.call-done = (f32[512,256]{1,0:T(8,128)}, f32[512,512]{1,0:T(8,128)}) async-done(((f32[512,256]{1,0:T(8,128)}, f32[512,512]{1,0:T(8,128)}), (f32[512,256]{1,0:T(8,128)}, f32[512,512]{1,0:T(8,128)})) %all-reduce.9.cloned.1.call-update) | async-done | bytes 1572880 | tf_op jit(solution)/shard_map/psum | solution.py:59
  333.3 72.5 %while.55 = (s32[]{:T(128)}, f32[512,256]{1,0:T(8,128)}, f32[512,256]{1,0:T(8,128)}, f32[512,256]{1,0:T(8,128)}, f32[]{:T(128)}, /*index=5*/f32[]{:T(128)}, f32[...) while((s32[]{:T(128)}, f32[512,256]{1,0:T(8,128)}, f32[512,256]{1,0:T(8,128)}, ...), condition=%wide.region_7.0_spmd, body=%wide.region_6.0_spmd.sunk | while | flops 805961728 | bytes 5243065 | solution.py:33
  334.4 3.7 fusion.58
  339.2 3.7 fusion.58
  344.1 3.7 fusion.58
  348.9 3.7 fusion.58
  353.7 3.7 fusion.58
  358.6 3.7 fusion.58
  363.4 3.7 fusion.58
  368.2 3.7 fusion.58
  373.1 3.7 fusion.58
  377.9 3.7 fusion.58
  382.7 3.7 fusion.58
  387.6 3.7 fusion.58
  397.2 3.7 fusion.58
  402.0 3.7 fusion.58
  415.2 102.8 %all-reduce.7.cloned.1.call-done = (f32[512,256]{1,0:T(8,128)}, f32[512,512]{1,0:T(8,128)}) async-done(((f32[512,256]{1,0:T(8,128)}, f32[512,512]{1,0:T(8,128)}), (f32[512,256]{1,0:T(8,128)}, f32[512,512]{1,0:T(8,128)})) %all-reduce.7.cloned.1.call-update) | async-done | bytes 1572880 | tf_op jit(solution)/shard_map/psum | solution.py:59
  522.6 70.1 %while.56 = (s32[]{:T(128)}, f32[512,256]{1,0:T(8,128)S(1)}, f32[512,256]{1,0:T(8,128)}, f32[512,256]{1,0:T(8,128)}, f32[]{:T(128)}, /*index=5*/f32[]{:T(128)}, ...) while((s32[]{:T(128)}, f32[512,256]{1,0:T(8,128)S(1)}, f32[512,256]{1,0:T(8,128)}, ...), condition=%wide.region_11.0_spmd, body=%wide.region_10.0_spmd.sunk | while | flops 805961728 | bytes 5243065 | solution.py:33
  592.7 4.3 convolution_subtract_fusion.3
  (136 shorter events, 199.2 us)
Async XLA Ops:
  7.2 4.3 copy-start
  7.2 134.1 %all-reduce.11.cloned.1.call-start = ((), (), s32[]{:S(2)}) async-start(), calls=%async_computation.2 | async-start | bytes 3145728 | tf_op jit(solution)/shard_map/psum | solution.py:59
  27.9 2.3 copy-start.8
  27.9 2.3 copy-start.9
  30.2 7.5 %copy-start.14 = (f32[3,2]{0,1:T(2,128)S(1)}, f32[3,2]{0,1:T(2,128)}, u32[]{:S(2)}) copy-start(f32[3,2]{0,1:T(2,128)} %param.16) | copy-start | bytes 76
  31.7 296.1 %all-reduce.9.cloned.1.call-start = ((), (), s32[]{:S(2)}) async-start(), calls=%async_computation.1 | async-start | bytes 3145728 | tf_op jit(solution)/shard_map/psum | solution.py:59
  57.4 1.3 copy-start.6
  141.3 2.8 copy-start.10
  216.0 4.1 copy-start.7
  218.8 1.3 copy-start.2
  221.7 296.4 %all-reduce.7.cloned.1.call-start = ((), (), s32[]{:S(2)}) async-start(), calls=%async_computation | async-start | bytes 3145728 | tf_op jit(solution)/shard_map/psum | solution.py:59
  241.1 1.3 copy-start.4
  327.8 3.6 copy-start.12
  329.8 0.8 copy-start.3
  405.7 4.6 copy-start.5
  409.0 1.3 copy-start.1
  518.1 2.8 copy-start.11
  597.0 0.6 copy-start.13
Sparse Core Ops, SparseCore 0:
  31.9 109.3 all-reduce.10
  221.8 105.9 all-reduce.8
  412.0 105.9 all-reduce.6
where the time goes:
time: 608 us; the launch traced here: 604 us
  waiting for transfers between devices  266 us (44%)
  matrix products  233 us (38%)
  local copies, waits for them, and re-layouts  59.8 us (10%)
  between operations  29.3 us (5%)
  other arithmetic  11.3 us (2%)
    psum x3, waiting for transfers between devices, body(): gram_sum, moment_sum = lax.psum((gram_part, moment_part), 'rows')  266 us
    dot_general x45, matrix products, apply_whole(): jnp.dot(gram, direction, precision=lax.Precision.HIGHEST, preferred_eleme...  162 us
    dot_general x3, matrix products, cosine_features(): jnp.dot(data, columns, preferred_element_type=jnp.float32) + shifts[None, :]  49.4 us
    while x45, local copies, waits for them, and re-layouts  46.9 us
  transfers between devices with their start and end apart: 3, of which 3 were waited for; matrix products, arithmetic and copies ran while one was open for 6% of the time, Pallas kernels for 0%

commit v1 on v0

v1 whole, which is shorter than its diff:
```python
import functools
import math

import jax
import jax.numpy as jnp
from jax import lax
from jax.experimental import pallas as pl
from jax.experimental.pallas import tpu as pltpu
from jax.sharding import PartitionSpec as P

F = 512
NBLK = 3
TILE = 256
SLAB = 16
BF = jnp.bfloat16
F32 = jnp.float32
TURN = 1.0 / (2.0 * math.pi)


def sine_coefficients(scale):
    import numpy as np

    nodes = np.cos((np.arange(64) + 0.5) * math.pi / 64)
    u = (nodes + 1) / 2 / 16
    a = np.sqrt(u)
    fit = np.polynomial.polynomial.polyfit(u, np.sin(2 * math.pi * a) / a, 4)
    return [float(c) * scale for c in fit]


def scaled_cosine(turns, coefficients):
    whole = jnp.round(turns)
    a = 0.25 - jnp.abs(turns - whole)
    u = a * a
    value = coefficients[-1]
    for c in coefficients[-2::-1]:
        value = value * u + c
    return value * a


def split(x):
    high = x.astype(BF)
    return high, (x - high.astype(F32)).astype(BF)


def dot3(left, right, dims=(((1,), (0,)), ((), ()))):
    lh, ll = left
    rh, rl = right
    dot = functools.partial(lax.dot_general, dimension_numbers=dims, preferred_element_type=F32)
    return dot(lh, rh) + (dot(lh, rl) + dot(ll, rh))


def features_kernel(coefficients, index, data, p0, p1, p2, h0, h1, h2, targets, feats, s_out, m_out, held):
    step = pl.program_id(0)

    @pl.when(step == 0)
    def _():
        s_out[...] = jnp.zeros_like(s_out)
        m_out[...] = jnp.zeros_like(m_out)

    x = data[...]
    y = targets[...]
    contract = (((0,), (0,)), ((), ()))
    for j, (p, h) in enumerate(((p0, h0), (p1, h1), (p2, h2))):
        angle = jnp.dot(x, p[...], preferred_element_type=F32)
        turns = angle * TURN + h[0] * TURN
        f = scaled_cosine(turns, coefficients).astype(BF)
        held[j] = f
        feats[:, j * F:(j + 1) * F] = f
        m_out[j * F:(j + 1) * F, :] += lax.dot_general(f, y, contract, preferred_element_type=F32)
    left = held[index[3]]
    other = held[index[4]]
    s_out[:, :F] += lax.dot_general(left, left, contract, preferred_element_type=F32)
    s_out[:, F:] += lax.dot_general(left, other, contract, preferred_element_type=F32)


def features_call(index, data, projections, phases, targets):
    rows = data.shape[0]
    classes = targets.shape[1]
    kernel = functools.partial(features_kernel, sine_coefficients(math.sqrt(2.0 / F)))

    def columns(j):
        return pl.BlockSpec((data.shape[1], F), lambda i, n: (0, n[j]))

    def shift(j):
        return pl.BlockSpec((1, 1, F), lambda i, n: (n[j], 0, 0))

    return pl.pallas_call(
        kernel,
        grid_spec=pltpu.PrefetchScalarGridSpec(
            num_scalar_prefetch=1,
            grid=(rows // TILE,),
            in_specs=[
                pl.BlockSpec((TILE, data.shape[1]), lambda i, n: (i, 0)),
                *[columns(j) for j in range(NBLK)],
                *[shift(j) for j in range(NBLK)],
                pl.BlockSpec((TILE, classes), lambda i, n: (i, 0)),
            ],
            out_specs=[
                pl.BlockSpec((TILE, NBLK * F), lambda i, n: (i, 0)),
                pl.BlockSpec((F, 2 * F), lambda i, n: (0, 0)),
                pl.BlockSpec((NBLK * F, classes), lambda i, n: (0, 0)),
            ],
            scratch_shapes=[pltpu.VMEM((NBLK, TILE, F), BF)],
        ),
        out_shape=[
            jax.ShapeDtypeStruct((rows, NBLK * F), BF),
            jax.ShapeDtypeStruct((F, 2 * F), F32),
            jax.ShapeDtypeStruct((NBLK * F, classes), F32),
        ],
        name="features",
    )(index, data, *[projections] * 3, *[phases.reshape(NBLK, 1, F)] * 3, targets)


def slabs_body(index, scale, s, out, s4):
    eye = (
        lax.broadcasted_iota(jnp.int32, (F, F), 0) == lax.broadcasted_iota(jnp.int32, (F, F), 1)
    ).astype(F32)
    first = s[:, :F] * scale[0] + eye * scale[1]
    part1 = split(first)
    second = scale[2] * (2.0 * first - dot3(part1, part1))
    part2 = split(second)
    fourth = scale[3] * (2.0 * second - dot3(part2, part2))
    part4 = split(fourth)
    s4[...] = fourth
    slab = s4[pl.ds(pl.multiple_of(index[0] * SLAB, SLAB), SLAB), :]
    row = lax.broadcasted_iota(jnp.int32, (SLAB, F), 0) + index[0] * SLAB
    column = lax.broadcasted_iota(jnp.int32, (SLAB, F), 1)
    unit = (row == column).astype(F32)
    eighth = scale[4] * (2.0 * slab - dot3(split(slab), part4))
    value = scale[5] * (2.0 * unit - eighth)
    value = scale[4] * (2.0 * value - dot3(split(value), part4))
    value = scale[3] * (2.0 * value - dot3(split(value), part2))
    value = scale[2] * (2.0 * value - dot3(split(value), part1))
    value = value * scale[6]
    out[0] = value
    out[1] = dot3(split(value), split(s[:, F:])) * scale[7]


def slabs_call(index, scale, s):
    smem = pl.BlockSpec(memory_space=pltpu.SMEM)
    return pl.pallas_call(
        slabs_body,
        in_specs=[smem, smem, pl.BlockSpec(memory_space=pltpu.VMEM)],
        out_specs=pl.BlockSpec(memory_space=pltpu.VMEM),
        out_shape=jax.ShapeDtypeStruct((2, SLAB, F), F32),
        scratch_shapes=[pltpu.VMEM((F, F), F32)],
        name="slabs",
    )(index, scale, s)


def solve_scales(lower, upper, total):
    center = 0.5 * (upper + lower)
    u = 0.5 * (upper - lower) / center
    factors = []
    for _ in range(4):
        factors.append(2.0 / (2.0 - u * u))
        u = u * u / (2.0 - u * u)
    return jnp.stack(
        [1.0 / (center * total), lower / center, *factors, 1.0 / center, jnp.full((), 1.0 / total, F32)]
    )


def body(data, projections, phases, targets, bounds, order):
    total = data.shape[0] * lax.axis_size("rows")
    me = lax.axis_index("rows").astype(jnp.int32)
    plane = lax.axis_index("cls").astype(jnp.int32)
    left = jnp.minimum(plane, 2)
    other = jnp.maximum(plane - 2, 0)
    index = jnp.concatenate([order.astype(jnp.int32), left[None], other[None]])
    feats, s, m = features_call(index, data, projections, phases, targets)
    s, m = lax.psum((s, m), "rows")
    bound = bounds[order[left]]
    scale = solve_scales(bound[0], bound[1], total)
    slabs = slabs_call(me[None], scale, s)
    slabs = lax.all_gather(slabs, "cls")
    m = (m * (1.0 / total)).reshape(NBLK, F, -1)
    dot = functools.partial(jnp.dot, precision=lax.Precision.HIGHEST, preferred_element_type=F32)
    gather = lambda w: lax.all_gather(w.astype(BF), "rows", axis=0, tiled=True)
    w0 = dot(slabs[0, 0], m[0])
    h0 = gather(w0)
    w1 = dot(slabs[1, 0], m[1]) - dot(slabs[1, 1], h0.astype(F32))
    h1 = gather(w1)
    w2 = dot(slabs[2, 0], m[2]) - dot(slabs[2, 1], h0.astype(F32)) - dot(slabs[3, 1], h1.astype(F32))
    h2 = gather(w2)
    half = jnp.concatenate([h0, h1, h2], axis=0)
    residual = targets.astype(F32) - jnp.dot(feats, half, preferred_element_type=F32)
    weights = jnp.zeros((NBLK,) + w0.shape, F32)
    for turn, w in enumerate((w0, w1, w2)):
        weights = lax.dynamic_update_slice(weights, w[None], (order[turn], jnp.int32(0), jnp.int32(0)))
    return (weights, residual)


def solution(mesh):
    return jax.shard_map(
        body,
        mesh=mesh,
        in_specs=(P("rows", None), P(), P(), P("rows", "cls"), P(), P()),
        out_specs=(P(None, "rows", "cls"), P("rows", "cls")),
        check_vma=False,
    )
```

time: 608 us -> 250 us (0.41)
  matrix products: 233 us -> 7.39 us
  waiting for transfers between devices: 266 us -> 99.7 us
  blocking collectives: 0 us -> 86.2 us
  local copies, waits for them, and re-layouts: 59.8 us -> 4 us
  Pallas kernels: 0 us -> 25.1 us
  other arithmetic: 11.3 us -> 1.41 us
    dot_general x57 -> x7, matrix products: 233 us -> 7.39 us  [the longest x1 5.95 us: body(): jnp.dot(feats, half, preferred_element_type=F32)]
    psum x3 -> x1, waiting for transfers between devices: 266 us -> 99.7 us  [body(): s, m = lax.psum((s, m), 'rows')]
    all_gather x0 -> x4, blocking collectives: none -> 86.2 us  [the longest x3 75.6 us: body(): gather = lambda w: lax.all_gather(w.astype(BF), 'rows', axis=0, tiled=True)]
    while x45 -> x0, local copies, waits for them, and re-layouts: 46.9 us -> none
    pallas_call x0 -> x2, Pallas kernels: none -> 25.1 us  [the longest x1 19.3 us: features_call(): pl.pallas_call(kernel, grid_spec=pltpu.PrefetchScalarGridSpec(num_scalar_...]
    unnamed x33 -> x10, local copies, waits for them, and re-layouts: 9.14 us -> 0.73 us
  transfers between devices with their start and end apart: 3 -> 1, of which waited for: 3 -> 1; matrix products, arithmetic and copies ran while one was open for 6% -> 1% of each run, Pallas kernels for 0% -> 0%
where the time goes in v1:
time: 250 us; the launch traced here: 249 us
  waiting for transfers between devices  99.7 us (40%)
  blocking collectives  86.2 us (34%)
  between operations  25.4 us (10%)
  Pallas kernels  25.1 us (10%)
  matrix products  7.39 us (3%)
  local copies, waits for them, and re-layouts  4 us (2%)
    psum x1, waiting for transfers between devices, body(): s, m = lax.psum((s, m), 'rows')  99.7 us
    all_gather x3, blocking collectives, body(): gather = lambda w: lax.all_gather(w.astype(BF), 'rows', axis=0, tiled=True)  75.6 us
    pallas_call x1, Pallas kernels, features_call(): pl.pallas_call(kernel, grid_spec=pltpu.PrefetchScalarGridSpec(num_scalar_...  19.3 us
    all_gather x1, blocking collectives, body(): slabs = lax.all_gather(slabs, 'cls')  10.6 us
    dot_general x1, matrix products, body(): jnp.dot(feats, half, preferred_element_type=F32)  5.95 us
    pallas_call x1, Pallas kernels, slabs_call(): pl.pallas_call(slabs_body, in_specs=[smem, smem, pl.BlockSpec(memory_spac...  5.78 us
  transfers between devices with their start and end apart: 1, of which 1 were waited for; matrix products, arithmetic and copies ran while one was open for 1% of the time, Pallas kernels for 0%

profile of v1, /device:TPU:1, one launch (start us, length us, event | category | flops | bytes accessed | tf_op | source)
XLA Modules:
  0.0 249.4 jit_solution(14999079852329606419)
XLA Ops:
  7.2 1.3 reshape.18.h0.h1.h2
  8.5 1.3 pad_add_fusion.index
  9.8 19.3 %features.1 = (bf16[2048,1536]{1,0:T(8,128)(2,1)}, f32[512,1024]{1,0:T(8,128)}, f32[1536,256]{1,0:T(8,128)}) custom-call(s32[5]{0:T(128)} %pad_add_fusion.index, bf16[2048,512]{1,0:T(8,128)(2,1)} %data.1, bf16[512,1536]{1,0:T(8,128)(2,1)} %p2.1, bf16[512,1536]{1,0:T(8,128)(2,1)} %p2.1, bf16[512,1536]{1,0:T(8,128)(2,1)} %p2.1, ...), custom_call_target="tpu_custom_call" | custom-call | tf_op jit(solution)/shard_map/features/pallas_call | solution.py:87
  29.2 0.6 copy-done.4
  29.9 0.7 fusion.13
  32.4 0.1 constant_dynamic-slice_fusion
  32.5 0.6 fusion.12
  42.5 0.6 stack.31.scale
  43.1 99.7 %all-reduce.3.cloned.1.call-done = (f32[1536,256]{1,0:T(8,128)}, f32[512,1024]{1,0:T(8,128)}) async-done(((f32[1536,256]{1,0:T(8,128)}, f32[512,1024]{1,0:T(8,128)}), (f32[1536,256]{1,0:T(8,128)}, f32[512,1024]{1,0:T(8,128)})) %all-reduce.3.cloned.1.call-update) | async-done | bytes 3670032 | tf_op jit(solution)/shard_map/psum | solution.py:171
  142.8 5.8 %slabs.1 = f32[2,16,512]{2,1,0:T(8,128)} custom-call(s32[1]{0:T(128)} %bitcast.index, f32[8]{0:T(128)} %stack.31.scale, f32[512,1024]{1,0:T(8,128)} %get-tuple-element.9.s), custom_call_target="tpu_custom_call" | custom-call | tf_op jit(solution)/shard_map/slabs/pallas_call | solution.py:141
  148.6 10.6 %all-gather = f32[8,16,512]{2,1,0:T(8,128)S(1)} all-gather(f32[2,16,512]{2,1,0:T(8,128)} %slabs.1), channel_id=2, replica_groups=mesh['rows'=32,'cls'=4] {'cls'}, dimensions={0}, use_global_device_ids=true | all-gather | bytes 327680 | tf_op jit(solution)/shard_map/all_gather | solution.py:175
  159.2 0.1 broadcast_multiply_fusion
  159.3 0.3 fusion.7
  159.6 0.0 copy-start.2
  159.7 0.3 fusion.5
  160.0 0.3 bitcast_dynamic-update-slice_fusion.2
  160.3 28.6 %all_gather.17 = bf16[512,256]{1,0:T(8,128)(2,1)S(1)} all-gather(bf16[16,256]{1,0:T(8,128)(2,1)S(1)} %get-tuple-element.17), channel_id=1, replica_groups=mesh['rows'=32,'cls'=4] {'rows'}, dimensions={0}, use_global_device_ids=true | all-gather | bytes 270336 | tf_op jit(solution)/shard_map/all_gather | solution.py:178
  188.9 0.2 bitcast_dynamic-update-slice_fusion.1
  189.0 22.2 %all_gather.18 = bf16[512,256]{1,0:T(8,128)(2,1)S(1)} all-gather(bf16[16,256]{1,0:T(8,128)(2,1)S(1)} %get-tuple-element.19), channel_id=1, replica_groups=mesh['rows'=32,'cls'=4] {'rows'}, dimensions={0}, use_global_device_ids=true | all-gather | bytes 270336 | tf_op jit(solution)/shard_map/all_gather | solution.py:178
  211.2 0.2 convolution_subtract_fusion.2
  211.4 0.2 bitcast_dynamic-update-slice_fusion
  211.6 0.0 copy-start.3
  211.7 24.9 %all_gather.19 = bf16[512,256]{1,0:T(8,128)(2,1)S(1)} all-gather(bf16[16,256]{1,0:T(8,128)(2,1)S(1)} %get-tuple-element.21), channel_id=1, replica_groups=mesh['rows'=32,'cls'=4] {'rows'}, dimensions={0}, use_global_device_ids=true | all-gather | bytes 270336 | tf_op jit(solution)/shard_map/all_gather | solution.py:178
  236.6 5.9 %convolution_subtract_fusion = f32[2048,256]{1,0:T(8,128)} fusion(bf16[2048,1536]{1,0:T(8,128)(2,1)} %get-tuple-element.7, bf16[2048,256]{1,0:T(8,128)(2,1)S(1)} %copy-done.2, bf16[512,256]{1,0:T(8,128)(2,1)S(1)} %all_gather.19, bf16[512,256]{1,0:T(8,128)(2,1)S(1)} %all_gather.18, bf16[512,256]{1,0:T(8,128)(2,1)S(1)} %all_gather.17), kind=kOutput, calls=%fused_computation | convolution fusion | flops 1614020608 | bytes 10223616 | tf_op jit(solution)/shard_map/dot_general | solution.py:186
  (10 shorter events, 0.1 us)
Async XLA Ops:
  7.2 25.2 %copy-start = (f32[3,2]{0,1:T(2,128)S(1)}, f32[3,2]{0,1:T(2,128)}, u32[]{:S(2)}) copy-start(f32[3,2]{0,1:T(2,128)} %param.10) | copy-start | bytes 76
  7.2 135.6 %all-reduce.3.cloned.1.call-start = ((), (), s32[]{:S(2)}) async-start(), calls=%async_computation | async-start | bytes 7340032 | tf_op jit(solution)/shard_map/psum | solution.py:171
  29.2 0.7 copy-start.4
  142.8 16.4 %copy-start.1 = (f32[1536,256]{1,0:T(8,128)S(1)}, f32[1536,256]{1,0:T(8,128)}, u32[]{:S(2)}) copy-start(f32[1536,256]{1,0:T(8,128)} %get-tuple-element.8) | copy-start | bytes 4718596
  159.6 77.0 %copy-start.2 = (bf16[2048,256]{1,0:T(8,128)(2,1)S(1)}, bf16[2048,256]{1,0:T(8,128)(2,1)}, u32[]{:S(2)}) copy-start(bf16[2048,256]{1,0:T(8,128)(2,1)} %targets.1) | copy-start | bytes 3145732
  211.6 30.9 %copy-start.3 = (f32[3,16,256]{2,1,0:T(8,128)}, f32[3,16,256]{2,1,0:T(8,128)S(1)}, u32[]{:S(2)}) copy-start(f32[3,16,256]{2,1,0:T(8,128)S(1)} %get-tuple-element.20) | copy-start | bytes 147460
Sparse Core Ops, SparseCore 0:
  29.3 113.4 all-reduce.2

commit v2 on v1

v2 whole, which is shorter than its diff:
```python
import functools
import math

import jax
import jax.numpy as jnp
from jax import lax
from jax.experimental import pallas as pl
from jax.experimental.pallas import tpu as pltpu
from jax.sharding import PartitionSpec as P

F = 512
NBLK = 3
TILE = 256
SLAB = 16
BF = jnp.bfloat16
F32 = jnp.float32
LANES = 128
ROWS = 32
PLANES = 4
GRAM, CROSS, MOMENT, HEIGHT = 0, 4 * F, 8 * F, 14 * F
TURN = 1.0 / (2.0 * math.pi)


def sine_coefficients(scale):
    import numpy as np

    nodes = np.cos((np.arange(64) + 0.5) * math.pi / 64)
    u = (nodes + 1) / 2 / 16
    a = np.sqrt(u)
    fit = np.polynomial.polynomial.polyfit(u, np.sin(2 * math.pi * a) / a, 4)
    return [float(c) * scale for c in fit]


def scaled_cosine(turns, coefficients):
    whole = jnp.round(turns)
    a = 0.25 - jnp.abs(turns - whole)
    u = a * a
    value = coefficients[-1]
    for c in coefficients[-2::-1]:
        value = value * u + c
    return value * a


def split(x):
    high = x.astype(BF)
    return high, (x - high.astype(F32)).astype(BF)


def dot3(left, right, dims=(((1,), (0,)), ((), ()))):
    lh, ll = left
    rh, rl = right
    dot = functools.partial(lax.dot_general, dimension_numbers=dims, preferred_element_type=F32)
    return dot(lh, rh) + (dot(lh, rl) + dot(ll, rh))


def features_kernel(coefficients, index, data, p0, p1, p2, h0, h1, h2, targets, feats, sums, held):
    step = pl.program_id(0)

    @pl.when(step == 0)
    def _():
        sums[...] = jnp.zeros_like(sums)

    x = data[...]
    y = targets[...]
    contract = (((0,), (0,)), ((), ()))

    def add(base, value):
        height, width = value.shape
        for k in range(width // LANES):
            rows = slice(base + k * height, base + (k + 1) * height)
            sums[rows, :] += value[:, k * LANES:(k + 1) * LANES]

    for j, (p, h) in enumerate(((p0, h0), (p1, h1), (p2, h2))):
        angle = jnp.dot(x, p[...], preferred_element_type=F32)
        turns = angle * TURN + h[0] * TURN
        f = scaled_cosine(turns, coefficients).astype(BF)
        held[j] = f
        feats[:, j * F:(j + 1) * F] = f
        add(MOMENT + 2 * F * j, lax.dot_general(f, y, contract, preferred_element_type=F32))
    left = held[index[3]]
    other = held[index[4]]
    add(GRAM, lax.dot_general(left, left, contract, preferred_element_type=F32))
    add(CROSS, lax.dot_general(left, other, contract, preferred_element_type=F32))


def features_call(index, data, projections, phases, targets):
    rows = data.shape[0]
    classes = targets.shape[1]
    kernel = functools.partial(features_kernel, sine_coefficients(math.sqrt(2.0 / F)))

    def columns(j):
        return pl.BlockSpec((data.shape[1], F), lambda i, n: (0, n[j]))

    def shift(j):
        return pl.BlockSpec((1, 1, F), lambda i, n: (n[j], 0, 0))

    return pl.pallas_call(
        kernel,
        grid_spec=pltpu.PrefetchScalarGridSpec(
            num_scalar_prefetch=1,
            grid=(rows // TILE,),
            in_specs=[
                pl.BlockSpec((TILE, data.shape[1]), lambda i, n: (i, 0)),
                *[columns(j) for j in range(NBLK)],
                *[shift(j) for j in range(NBLK)],
                pl.BlockSpec((TILE, classes), lambda i, n: (i, 0)),
            ],
            out_specs=[
                pl.BlockSpec((TILE, NBLK * F), lambda i, n: (i, 0)),
                pl.BlockSpec((HEIGHT, LANES), lambda i, n: (0, 0)),
            ],
            scratch_shapes=[pltpu.VMEM((NBLK, TILE, F), BF)],
        ),
        out_shape=[
            jax.ShapeDtypeStruct((rows, NBLK * F), BF),
            jax.ShapeDtypeStruct((HEIGHT, LANES), F32),
        ],
        name="features",
    )(index, data, *[projections] * 3, *[phases.reshape(NBLK, 1, F)] * 3, targets)


CHUNKS = ((GRAM, 4 * F), (CROSS, 4 * F), (MOMENT, 6 * F))
COPIES = 51


def mod4(v):
    return lax.rem(v + 8, 4)


class Place:
    def __init__(self):
        self.row = lax.axis_index("rows")
        self.plane = lax.axis_index("cls")
        self.core = lax.rem(self.row, 2)
        self.x = lax.rem(lax.div(self.row, 2), 4)
        self.y = lax.div(self.row, 8)
        self.partner = {"rows": self.row + 1 - 2 * self.core}

    def at(self, axis):
        return self.x if axis == "x" else self.y

    def near(self, axis, step):
        x = mod4(self.x + step) if axis == "x" else self.x
        y = mod4(self.y + step) if axis == "y" else self.y
        return {"rows": (y * 4 + x) * 2 + self.core}


def window(start, size):
    return pl.ds(pl.multiple_of(start, 8), size)


def reduce_chunk(place, q, base, height, v, out, r0, acc, ring1, ring2, part1, send_sem, recv_sem, copies):
    half = height // 2

    def send(k, source, target, device):
        copy = pltpu.make_async_remote_copy(
            src_ref=source, dst_ref=target, send_sem=send_sem.at[q, k], recv_sem=recv_sem.at[q, k],
            device_id=device, device_id_type=pl.DeviceIdType.MESH,
        )
        copy.start()
        copies.append(copy)
        return copy

    first = send(0, v.at[window(base + (1 - place.core) * half, half)], r0, place.partner)
    yield
    first.wait_recv()
    acc[...] = v[window(base + place.core * half, half), :] + r0[...]
    ways = [(part, h) for part in range(2) for h in range(2)]
    sign = (1, -1)

    def scatter(k, axes, source, origin, size, ring, store):
        small = size // 2

        def piece(part, i, h):
            return window(origin(part) + i * size + h * small, small)

        far, close, on = {}, {}, {}
        for part, h in ways:
            axis, s = axes[part], sign[h]
            i = place.at(axis)
            n = part * 2 + h
            far[n] = send(k + n, source.at[piece(part, mod4(i + 2), h)], ring.at[n, 0], place.near(axis, s))
            close[n] = send(k + 4 + n, source.at[piece(part, mod4(i - s), h)], ring.at[n, 1], place.near(axis, -s))
        yield
        for part, h in ways:
            axis, s = axes[part], sign[h]
            i = place.at(axis)
            n = part * 2 + h
            far[n].wait_recv()
            ring[n, 3] = source[piece(part, mod4(i + s), h), :] + ring[n, 0]
            on[n] = send(k + 8 + n, ring.at[n, 3], ring.at[n, 2], place.near(axis, s))
        yield
        for part, h in ways:
            i = place.at(axes[part])
            n = part * 2 + h
            close[n].wait_recv()
            on[n].wait_recv()
            store(part, h, source[piece(part, i, h), :] + ring[n, 1] + ring[n, 2])

    def gather(k, axes, origin, size):
        small = size // 2

        def piece(part, i, h):
            return out.at[window(base + origin(part) + i * size + h * small, small)]

        ahead, back, on = {}, {}, {}
        for part, h in ways:
            axis, s = axes[part], sign[h]
            n = part * 2 + h
            mine = piece(part, place.at(axis), h)
            ahead[n] = send(k + n, mine, mine, place.near(axis, s))
            back[n] = send(k + 4 + n, mine, mine, place.near(axis, -s))
        yield
        for part, h in ways:
            axis, s = axes[part], sign[h]
            n = part * 2 + h
            ahead[n].wait_recv()
            theirs = piece(part, mod4(place.at(axis) - s), h)
            on[n] = send(k + 8 + n, theirs, theirs, place.near(axis, s))
        yield
        for n in range(4):
            back[n].wait_recv()
            on[n].wait_recv()

    one, two = ("x", "y"), ("y", "x")
    quarter, sixteenth, last = height // 4, height // 16, height // 64

    def store1(part, h, value):
        part1[part * sixteenth + h * (sixteenth // 2):part * sixteenth + (h + 1) * (sixteenth // 2), :] = value

    yield from scatter(1, one, acc, lambda part: part * quarter, sixteenth, ring1, store1)

    def own(part):
        return place.core * half + part * quarter + place.at(one[part]) * sixteenth

    def store2(part, h, value):
        start = base + own(part) + place.at(two[part]) * last + h * (last // 2)
        out[window(start, last // 2), :] = value

    yield from scatter(13, two, part1, lambda part: part * sixteenth, last, ring2, store2)
    yield from gather(25, two, own, last)
    yield from gather(37, one, lambda part: place.core * half + part * quarter, sixteenth)
    finals = []
    for part in range(2):
        mine = out.at[window(base + place.core * half + part * quarter, quarter)]
        finals.append(send(49 + part, mine, mine, place.partner))
    yield
    for copy in finals:
        copy.wait_recv()


def exchange_kernel(scale, v, w_out, wh_out, out, s4, slabs, *scratch):
    place = Place()
    buffers, (send_sem, recv_sem, plane_send, plane_recv, wide_send, wide_recv) = scratch[:-6], scratch[-6:]
    me, plane = place.row, place.plane
    barrier = pltpu.get_barrier_semaphore()

    def greet(d, carry):
        pl.semaphore_signal(
            barrier, inc=1, device_id={"rows": lax.rem(me + d, ROWS)}, device_id_type=pl.DeviceIdType.MESH
        )
        return carry

    lax.fori_loop(1, ROWS, greet, 0)
    for d in range(1, PLANES):
        pl.semaphore_signal(
            barrier, inc=1, device_id={"cls": lax.rem(plane + d, PLANES)}, device_id_type=pl.DeviceIdType.MESH
        )
    pl.semaphore_wait(barrier, ROWS - 1 + PLANES - 1)

    copies = []
    runs = []
    for q, (base, height) in enumerate(CHUNKS):
        runs.append(reduce_chunk(place, q, base, height, v, out, *buffers[5 * q:5 * q + 5], send_sem, recv_sem, copies))
    done = [False] * len(runs)

    def advance(q):
        if not done[q]:
            try:
                next(runs[q])
            except StopIteration:
                done[q] = True

    lead = 0
    while not all(done[:2]):
        for q in range(min(lead + 1, len(runs))):
            advance(q)
        lead += 1

    def wide(base, width):
        return jnp.concatenate([out[base + k * F:base + (k + 1) * F, :] for k in range(width // LANES)], axis=1)

    eye = (
        lax.broadcasted_iota(jnp.int32, (F, F), 0) == lax.broadcasted_iota(jnp.int32, (F, F), 1)
    ).astype(F32)
    first = wide(GRAM, F) * scale[0] + eye * scale[1]
    part1 = split(first)
    second = scale[2] * (2.0 * first - dot3(part1, part1))
    advance(2)
    part2 = split(second)
    fourth = scale[3] * (2.0 * second - dot3(part2, part2))
    advance(2)
    part4 = split(fourth)
    s4[...] = fourth
    slab = s4[window(me * SLAB, SLAB), :]
    row = lax.broadcasted_iota(jnp.int32, (SLAB, F), 0) + me * SLAB
    column = lax.broadcasted_iota(jnp.int32, (SLAB, F), 1)
    unit = (row == column).astype(F32)
    eighth = scale[4] * (2.0 * slab - dot3(split(slab), part4))
    value = scale[5] * (2.0 * unit - eighth)
    value = scale[4] * (2.0 * value - dot3(split(value), part4))
    advance(2)
    value = scale[3] * (2.0 * value - dot3(split(value), part2))
    value = scale[2] * (2.0 * value - dot3(split(value), part1))
    value = value * scale[0]
    slabs[plane, 0] = value
    slabs[plane, 1] = dot3(split(value), split(wide(CROSS, F)))
    across = []
    for d in range(1, PLANES):
        copy = pltpu.make_async_remote_copy(
            src_ref=slabs.at[plane], dst_ref=slabs.at[plane], send_sem=plane_send.at[d], recv_sem=plane_recv.at[d],
            device_id={"cls": lax.rem(plane + d, PLANES)}, device_id_type=pl.DeviceIdType.MESH,
        )
        copy.start()
        across.append(copy)
    while not done[2]:
        advance(2)
    for copy in across:
        copy.wait_recv()

    def moment(j):
        return split(wide(MOMENT + 2 * F * j, 2 * LANES))

    def product(z, k, right):
        return dot3(split(slabs[z, k]), right)

    def product2(z, k, right):
        high, low = split(slabs[z, k])
        return jnp.dot(high, right, preferred_element_type=F32) + jnp.dot(low, right, preferred_element_type=F32)

    def broadcast(j, w):
        w_out[j] = w
        mine = wh_out.at[j, pl.ds(pl.multiple_of(me * SLAB, SLAB), SLAB)]
        wh_out[j, pl.ds(pl.multiple_of(me * SLAB, SLAB), SLAB), :] = w.astype(BF)

        def tell(d, carry):
            pltpu.make_async_remote_copy(
                src_ref=mine, dst_ref=mine, send_sem=wide_send.at[j], recv_sem=wide_recv.at[j],
                device_id={"rows": lax.rem(me + d, ROWS)}, device_id_type=pl.DeviceIdType.MESH,
            ).start()
            return carry

        lax.fori_loop(1, ROWS, tell, 0)

    def all_but_one(j):
        part = wh_out.at[j, pl.ds(0, (ROWS - 1) * SLAB)]
        return pltpu.make_async_remote_copy(
            src_ref=part, dst_ref=part, send_sem=wide_send.at[j], recv_sem=wide_recv.at[j],
            device_id=place.partner, device_id_type=pl.DeviceIdType.MESH,
        )

    broadcast(0, product(0, 0, moment(0)))
    w1 = product(1, 0, moment(1))
    w2 = product(2, 0, moment(2))
    all_but_one(0).wait_recv()
    broadcast(1, w1 - product2(1, 1, wh_out[0]))
    w2 = w2 - product2(2, 1, wh_out[0])
    all_but_one(1).wait_recv()
    broadcast(2, w2 - product2(3, 1, wh_out[1]))
    all_but_one(2).wait_recv()
    for copy in copies + across:
        copy.wait_send()
    for j in range(NBLK):
        all_but_one(j).wait_send()


def exchange_call(scale, sums, classes):
    vmem = pl.BlockSpec(memory_space=pltpu.VMEM)
    buffers = []
    for _, height in CHUNKS:
        buffers += [
            pltpu.VMEM((height // 2, LANES), F32),
            pltpu.VMEM((height // 2, LANES), F32),
            pltpu.VMEM((4, 4, height // 32, LANES), F32),
            pltpu.VMEM((4, 4, height // 128, LANES), F32),
            pltpu.VMEM((height // 8, LANES), F32),
        ]
    dma = pltpu.SemaphoreType.DMA
    return pl.pallas_call(
        exchange_kernel,
        in_specs=[pl.BlockSpec(memory_space=pltpu.SMEM), vmem],
        out_specs=[vmem, vmem],
        out_shape=[
            jax.ShapeDtypeStruct((NBLK, SLAB, classes), F32),
            jax.ShapeDtypeStruct((NBLK, F, classes), BF),
        ],
        scratch_shapes=[
            pltpu.VMEM((HEIGHT, LANES), F32),
            pltpu.VMEM((F, F), F32),
            pltpu.VMEM((PLANES, 2, SLAB, F), F32),
            *buffers,
            dma((len(CHUNKS), COPIES)),
            dma((len(CHUNKS), COPIES)),
            dma((PLANES,)),
            dma((PLANES,)),
            dma((NBLK,)),
            dma((NBLK,)),
        ],
        compiler_params=pltpu.CompilerParams(collective_id=0, has_side_effects=True),
        name="exchange",
    )(scale, sums)


def solve_scales(lower, upper, total):
    center = 0.5 * (upper + lower)
    u = 0.5 * (upper - lower) / center
    factors = []
    for _ in range(4):
        factors.append(2.0 / (2.0 - u * u))
        u = u * u / (2.0 - u * u)
    return jnp.stack([1.0 / (center * total), lower / center, *factors])


def body(data, projections, phases, targets, bounds, order):
    total = data.shape[0] * lax.axis_size("rows")
    plane = lax.axis_index("cls").astype(jnp.int32)
    left = jnp.minimum(plane, 2)
    other = jnp.maximum(plane - 2, 0)
    index = jnp.concatenate([order.astype(jnp.int32), left[None], other[None]])
    feats, sums = features_call(index, data, projections, phases, targets)
    bound = bounds[order[left]]
    scale = solve_scales(bound[0], bound[1], total)
    w, half = exchange_call(scale, sums, targets.shape[1])
    half = half.reshape(NBLK * F, -1)
    residual = targets.astype(F32) - jnp.dot(feats, half, preferred_element_type=F32)
    weights = jnp.zeros(w.shape, F32)
    for turn in range(NBLK):
        weights = lax.dynamic_update_slice(weights, w[turn][None], (order[turn], jnp.int32(0), jnp.int32(0)))
    return (weights, residual)


def solution(mesh):
    return jax.shard_map(
        body,
        mesh=mesh,
        in_specs=(P("rows", None), P(), P(), P("rows", "cls"), P(), P()),
        out_specs=(P(None, "rows", "cls"), P("rows", "cls")),
        check_vma=False,
    )
```

time: 250 us -> 127 us (0.51)
  waiting for transfers between devices: 99.7 us -> 0 us
  blocking collectives: 86.2 us -> 0 us
  Pallas kernels: 25.1 us -> 103 us
  between operations: 25.4 us -> 11.6 us
    psum x1 -> x0, waiting for transfers between devices: 99.7 us -> none  [body(): s, m = lax.psum((s, m), 'rows')]
    all_gather x4 -> x0, blocking collectives: 86.2 us -> none  [the longest x3 75.6 us: body(): gather = lambda w: lax.all_gather(w.astype(BF), 'rows', axis=0, tiled=True)]
    pallas_call x1, Pallas kernels: 5.78 us -> 83.5 us  [exchange_call(): pl.pallas_call(exchange_kernel, in_specs=[pl.BlockSpec(memory_space=pltpu...]
  transfers between devices with their start and end apart: 1 -> 0, of which waited for: 1 -> 0; matrix products, arithmetic and copies ran while one was open for 1% -> 0% of each run, Pallas kernels for 0% -> 0%
where the time goes in v2:
time: 127 us
  Pallas kernels  103 us (81%)
  between operations  11.6 us (9%)
  matrix products  6.12 us (5%)
  local copies, waits for them, and re-layouts  4.64 us (4%)
    pallas_call x1, Pallas kernels, exchange_call(): pl.pallas_call(exchange_kernel, in_specs=[pl.BlockSpec(memory_space=pltpu...  83.5 us
    pallas_call x1, Pallas kernels, features_call(): pl.pallas_call(kernel, grid_spec=pltpu.PrefetchScalarGridSpec(num_scalar_...  19.6 us
    dot_general x1, matrix products, body(): jnp.dot(feats, half, preferred_element_type=F32)  6.12 us

profile of v2, /device:TPU:1, one launch (start us, length us, event | category | flops | bytes accessed | tf_op | source)
XLA Modules:
  0.0 126.7 jit_solution(98879424944972337)
XLA Ops:
  0.6 0.0 copy-start
  0.7 1.5 %fusion.1 = (s32[1]{0:T(128)}, s32[1]{0:T(128)}, s32[1]{0:T(128)}, s32[1]{0:T(128)}) fusion(s32[3]{0:T(128)} %param.11, s32[]{:T(128)S(6)} %select_n.15), kind=kLoop, calls=%fused_computation.7 | loop fusion | bytes 36 | tf_op jit(solution)/shard_map/slice | solution.py:438
  4.1 0.0 copy-done
  4.1 0.1 constant_dynamic-slice_fusion
  4.1 0.5 fusion
  8.1 0.6 stack.27.scale
  8.7 1.2 pad_add_fusion.index
  9.9 1.3 %reshape.14.h0.h1.h2 = f32[3,1,512]{2,1,0:T(1,128)} reshape(f32[1536]{0:T(1024)} %param.8) | data formatting | bytes 12288 | tf_op jit(solution)/shard_map/reshape | solution.py:119
  11.2 19.6 %features.1 = (bf16[2048,1536]{1,0:T(8,128)(2,1)}, f32[7168,128]{1,0:T(8,128)}) custom-call(s32[5]{0:T(128)} %pad_add_fusion.index, bf16[2048,512]{1,0:T(8,128)(2,1)} %data.1, bf16[512,1536]{1,0:T(8,128)(2,1)} %p2.1, bf16[512,1536]{1,0:T(8,128)(2,1)} %p2.1, bf16[512,1536]{1,0:T(8,128)(2,1)} %p2.1, f32[3,1,512]{2,1,0:T(1,128)} %reshape.14.h0.h1.h2, ...), custom_call_target="tpu_custom_call" | custom-call | tf_op jit(solution)/shard_map/features/pallas_call | solution.py:97
  30.8 0.0 copy-start.1
  30.8 83.5 %exchange.1 = (f32[3,16,256]{2,1,0:T(8,128)}, bf16[3,512,256]{2,1,0:T(8,128)(2,1)}) custom-call(f32[6]{0:T(128)} %stack.27.scale, f32[7168,128]{1,0:T(8,128)} %get-tuple-element.6.v), custom_call_target="tpu_custom_call" | custom-call | tf_op jit(solution)/shard_map/exchange/pallas_call | solution.py:389
  114.4 0.0 copy-done.1
  114.4 0.0 copy-start.3
  114.4 6.1 %convolution_subtract_fusion = f32[2048,256]{1,0:T(8,128)} fusion(bf16[2048,1536]{1,0:T(8,128)(2,1)} %get-tuple-element.8, bf16[1536,256]{1,0:T(8,128)(2,1)} %bitcast.17, bf16[2048,256]{1,0:T(8,128)(2,1)S(1)} %copy-done.1), kind=kOutput, calls=%fused_computation | convolution fusion | flops 1611661312 | bytes 10223616 | tf_op jit(solution)/shard_map/dot_general | solution.py:435
  122.2 0.0 copy-done.3
  126.1 0.0 copy-start.2
  126.1 0.6 copy-done.2
  (4 shorter events, 0.0 us)
Async XLA Ops:
  0.6 3.4 %copy-start = (f32[3,2]{0,1:T(2,128)S(1)}, f32[3,2]{0,1:T(2,128)}, u32[]{:S(2)}) copy-start(f32[3,2]{0,1:T(2,128)} %param.10) | copy-start | bytes 76
  30.8 83.5 %copy-start.1 = (bf16[2048,256]{1,0:T(8,128)(2,1)S(1)}, bf16[2048,256]{1,0:T(8,128)(2,1)}, u32[]{:S(2)}) copy-start(bf16[2048,256]{1,0:T(8,128)(2,1)} %targets.1) | copy-start | bytes 3145732
  114.4 7.8 %copy-start.3 = (f32[3,16,256]{2,1,0:T(8,128)S(1)}, f32[3,16,256]{2,1,0:T(8,128)}, u32[]{:S(2)}) copy-start(f32[3,16,256]{2,1,0:T(8,128)} %get-tuple-element.7) | copy-start | bytes 147460
  126.1 0.6 copy-start.2

commit v3 on v2

v3 whole, which is shorter than its diff:
```python
import functools
import math

import jax
import jax.numpy as jnp
from jax import lax
from jax.experimental import pallas as pl
from jax.experimental.pallas import tpu as pltpu
from jax.sharding import PartitionSpec as P

F = 512
NBLK = 3
TILE = 512
RESIDUAL_TILE = 256
TILES = 4
SLAB = 16
BF = jnp.bfloat16
F32 = jnp.float32
LANES = 128
ROWS = 32
PLANES = 4
GRAM, CROSS, MOMENT, HEIGHT = 0, 4 * F, 8 * F, 14 * F
TURN = 1.0 / (2.0 * math.pi)


def sine_coefficients(scale):
    import numpy as np

    nodes = np.cos((np.arange(64) + 0.5) * math.pi / 64)
    u = (nodes + 1) / 2 / 16
    a = np.sqrt(u)
    fit = np.polynomial.polynomial.polyfit(u, np.sin(2 * math.pi * a) / a, 3, w=a)
    return [float(c) * scale for c in fit]


def scaled_cosine(turns, coefficients):
    a = 0.25 - jnp.abs(turns - jnp.round(turns))
    u = a * a
    value = coefficients[-1]
    for c in coefficients[-2::-1]:
        value = value * u + c
    return value * a


def split(x):
    high = x.astype(BF)
    return high, (x - high.astype(F32)).astype(BF)


def dot3(left, right, dims=(((1,), (0,)), ((), ()))):
    lh, ll = left
    rh, rl = right
    dot = functools.partial(lax.dot_general, dimension_numbers=dims, preferred_element_type=F32)
    return dot(lh, rh) + (dot(lh, rl) + dot(ll, rh))


def mod4(v):
    return lax.rem(v + 8, 4)


class Place:
    def __init__(self):
        self.row = lax.axis_index("rows")
        self.plane = lax.axis_index("cls")
        self.core = lax.rem(self.row, 2)
        self.x = lax.rem(lax.div(self.row, 2), 4)
        self.y = lax.div(self.row, 8)
        self.partner = {"rows": self.row + 1 - 2 * self.core}

    def at(self, axis):
        return self.x if axis == "x" else self.y

    def near(self, axis, step):
        x = mod4(self.x + step) if axis == "x" else self.x
        y = mod4(self.y + step) if axis == "y" else self.y
        return {"rows": (y * 4 + x) * 2 + self.core}


def window(start, size):
    return pl.ds(pl.multiple_of(start, 8), size)


CHUNKS = (
    (GRAM, 4 * F, (True, True, True, True)),
    (CROSS, 4 * F, (True, True, True, True)),
    (MOMENT, 6 * F, (False, True, True, False)),
)
COPIES = 51


def ring_shape(size, direct):
    return (2, 3, size, LANES) if direct else (4, 4, size // 2, LANES)


def reduce_chunk(place, q, v, out, r0, acc, ring1, ring2, part1, send_sem, recv_sem, copies):
    base, height, direct = CHUNKS[q]
    half = height // 2
    ways = [(part, h) for part in range(2) for h in range(2)]
    hops = [(part, d) for part in range(2) for d in range(1, 4)]
    sign = (1, -1)

    def send(k, source, target, device):
        copy = pltpu.make_async_remote_copy(
            src_ref=source, dst_ref=target, send_sem=send_sem.at[q, k], recv_sem=recv_sem.at[q, k],
            device_id=device, device_id_type=pl.DeviceIdType.MESH,
        )
        copy.start()
        copies.append(copy)
        return copy

    first = send(0, v.at[window(base + (1 - place.core) * half, half)], r0, place.partner)
    yield
    first.wait_recv()
    acc[...] = v[window(base + place.core * half, half), :] + r0[...]

    def scatter_direct(k, axes, source, origin, size, ring, store):
        flights = {}
        for part, d in sorted(hops, key=lambda hop: hop[1] != 2):
            target = mod4(place.at(axes[part]) + d)
            piece = source.at[window(origin(part) + target * size, size)]
            flights[part, d] = send(k + part * 3 + d - 1, piece, ring.at[part, d - 1], place.near(axes[part], d))
        yield
        for part in range(2):
            total = source[window(origin(part) + place.at(axes[part]) * size, size), :]
            for d in range(1, 4):
                flights[part, d].wait_recv()
                total = total + ring[part, d - 1]
            store(part, 0, total)

    def gather_direct(k, axes, origin, size):
        flights = []
        for part, d in sorted(hops, key=lambda hop: hop[1] != 2):
            mine = out.at[window(base + origin(part) + place.at(axes[part]) * size, size)]
            flights.append(send(k + part * 3 + d - 1, mine, mine, place.near(axes[part], d)))
        yield
        for copy in flights:
            copy.wait_recv()

    def scatter_ring(k, axes, source, origin, size, ring, store):
        small = size // 2

        def piece(part, i, h):
            return window(origin(part) + i * size + h * small, small)

        far, close, on = {}, {}, {}
        for part, h in ways:
            axis, s = axes[part], sign[h]
            i = place.at(axis)
            n = part * 2 + h
            far[n] = send(k + n, source.at[piece(part, mod4(i + 2), h)], ring.at[n, 0], place.near(axis, s))
            close[n] = send(k + 4 + n, source.at[piece(part, mod4(i - s), h)], ring.at[n, 1], place.near(axis, -s))
        yield
        for part, h in ways:
            axis, s = axes[part], sign[h]
            i = place.at(axis)
            n = part * 2 + h
            far[n].wait_recv()
            ring[n, 3] = source[piece(part, mod4(i + s), h), :] + ring[n, 0]
            on[n] = send(k + 8 + n, ring.at[n, 3], ring.at[n, 2], place.near(axis, s))
        yield
        for part, h in ways:
            i = place.at(axes[part])
            n = part * 2 + h
            close[n].wait_recv()
            on[n].wait_recv()
            store(part, h, source[piece(part, i, h), :] + ring[n, 1] + ring[n, 2])

    def gather_ring(k, axes, origin, size):
        small = size // 2

        def piece(part, i, h):
            return out.at[window(base + origin(part) + i * size + h * small, small)]

        ahead, back, on = {}, {}, {}
        for part, h in ways:
            axis, s = axes[part], sign[h]
            n = part * 2 + h
            mine = piece(part, place.at(axis), h)
            ahead[n] = send(k + n, mine, mine, place.near(axis, s))
            back[n] = send(k + 4 + n, mine, mine, place.near(axis, -s))
        yield
        for part, h in ways:
            axis, s = axes[part], sign[h]
            n = part * 2 + h
            ahead[n].wait_recv()
            theirs = piece(part, mod4(place.at(axis) - s), h)
            on[n] = send(k + 8 + n, theirs, theirs, place.near(axis, s))
        yield
        for n in range(4):
            back[n].wait_recv()
            on[n].wait_recv()

    def pick(straight, ringed, stage):
        return straight if direct[stage] else ringed

    one, two = ("x", "y"), ("y", "x")
    quarter, sixteenth, last = height // 4, height // 16, height // 64

    def store1(part, h, value):
        start = part * sixteenth + h * value.shape[0]
        part1[start:start + value.shape[0], :] = value

    scatter = pick(scatter_direct, scatter_ring, 0)
    yield from scatter(1, one, acc, lambda part: part * quarter, sixteenth, ring1, store1)

    def own(part):
        return place.core * half + part * quarter + place.at(one[part]) * sixteenth

    def store2(part, h, value):
        start = base + own(part) + place.at(two[part]) * last + h * value.shape[0]
        out[window(start, value.shape[0]), :] = value

    scatter = pick(scatter_direct, scatter_ring, 1)
    yield from scatter(13, two, part1, lambda part: part * sixteenth, last, ring2, store2)
    yield from pick(gather_direct, gather_ring, 2)(25, two, own, last)
    gather = pick(gather_direct, gather_ring, 3)
    yield from gather(37, one, lambda part: place.core * half + part * quarter, sixteenth)
    finals = []
    for part in range(2):
        mine = out.at[window(base + place.core * half + part * quarter, quarter)]
        finals.append(send(49 + part, mine, mine, place.partner))
    yield
    for copy in finals:
        copy.wait_recv()


def exchange_kernel(
    coefficients, order, bounds, phases, data_in, proj_in, targets_in, w_out, wh_out, feats_out,
    data, proj, chosen, targets, feats, v, out, s4, slabs, *scratch
):
    place = Place()
    buffers = scratch[:5 * len(CHUNKS)]
    send_sem, recv_sem, plane_send, plane_recv, wide_send, wide_recv, load_sem, store_sem = scratch[5 * len(CHUNKS):]
    me, plane = place.row, place.plane
    height = data.shape[0]
    loads = [pltpu.make_async_copy(proj_in, proj, load_sem.at[0])]
    for t in range(TILES):
        rows = pl.ds(t * TILE, TILE)
        loads.append(pltpu.make_async_copy(data_in.at[rows], data.at[rows], load_sem.at[1 + t]))
    loads.append(pltpu.make_async_copy(targets_in, targets, load_sem.at[1 + TILES]))
    for copy in loads:
        copy.start()

    barrier = pltpu.get_barrier_semaphore()

    def greet(d, carry):
        pl.semaphore_signal(
            barrier, inc=1, device_id={"rows": lax.rem(me + d, ROWS)}, device_id_type=pl.DeviceIdType.MESH
        )
        return carry

    lax.fori_loop(1, ROWS, greet, 0)
    for d in range(1, PLANES):
        pl.semaphore_signal(
            barrier, inc=1, device_id={"cls": lax.rem(plane + d, PLANES)}, device_id_type=pl.DeviceIdType.MESH
        )

    copies = []
    runs = [
        reduce_chunk(place, q, v, out, *buffers[5 * q:5 * q + 5], send_sem, recv_sem, copies)
        for q in range(len(CHUNKS))
    ]
    done = [False] * len(runs)

    def advance(*which):
        for q in which:
            if not done[q]:
                try:
                    next(runs[q])
                except StopIteration:
                    done[q] = True

    turn_a = jnp.minimum(plane, 2)
    turn_b = jnp.where(plane == 0, 1, jnp.where(plane == 3, 1, 0))
    turn_c = 3 - turn_a - turn_b
    contract = (((0,), (0,)), ((), ()))

    def pick(turn, values):
        block = order[turn]
        return jnp.where(block == 0, values[0], jnp.where(block == 1, values[1], values[2]))

    def columns(ref):
        return [ref[:, j * F:(j + 1) * F] for j in range(NBLK)]

    def choose(turn):
        chosen[...] = pick(turn, columns(proj))

    def features(turn, tiles):
        shift = pick(turn, columns(phases)) * TURN
        for t in tiles:
            rows = pl.ds(t * TILE, TILE)
            angle = jnp.dot(data[rows, :], chosen[...], preferred_element_type=F32)
            feats[turn, rows, :] = scaled_cosine(angle * TURN + shift, coefficients).astype(BF)

    def put(base, value):
        tall, width = value.shape
        for k in range(width // LANES):
            v[window(base + k * tall, tall), :] = value[:, k * LANES:(k + 1) * LANES]

    def keep(n, turn):
        copy = pltpu.make_async_copy(feats.at[turn], feats_out.at[turn], store_sem.at[n])
        copy.start()
        return copy

    def moments(turn):
        put(MOMENT + 2 * F * turn, lax.dot_general(feats[turn], targets[...], contract, preferred_element_type=F32))

    loads[0].wait()
    for t in range(TILES):
        loads[1 + t].wait()
    choose(turn_a)
    features(turn_a, range(TILES))
    put(GRAM, lax.dot_general(feats[turn_a], feats[turn_a], contract, preferred_element_type=F32))
    pl.semaphore_wait(barrier, ROWS - 1 + PLANES - 1)
    advance(0)
    choose(turn_b)
    features(turn_b, range(2))
    advance(0)
    features(turn_b, range(2, TILES))
    put(CROSS, lax.dot_general(feats[turn_a], feats[turn_b], contract, preferred_element_type=F32))
    advance(0, 1)
    choose(turn_c)
    features(turn_c, range(2))
    advance(0, 1)
    features(turn_c, range(2, TILES))
    advance(0)
    loads[1 + TILES].wait()
    for turn in (turn_a, turn_b, turn_c):
        moments(turn)
    advance(0, 1, 2)
    stores = [keep(n, turn) for n, turn in enumerate((turn_a, turn_b, turn_c))]
    while not done[0]:
        advance(0, 1, 2)

    def wide(base, width):
        return jnp.concatenate([out[window(base + k * F, F), :] for k in range(width // LANES)], axis=1)

    lower = jnp.full((1, F), pick(turn_a, [bounds[j, 0] for j in range(NBLK)]), F32)
    upper = jnp.full((1, F), pick(turn_a, [bounds[j, 1] for j in range(NBLK)]), F32)
    center = 0.5 * (upper + lower)
    u = 0.5 * (upper - lower) / center
    k1 = 2.0 / (2.0 - u * u)
    u = u * u / (2.0 - u * u)
    k2 = 2.0 / (2.0 - u * u)
    u = u * u / (2.0 - u * u)
    k4 = 2.0 / (2.0 - u * u)
    u = u * u / (2.0 - u * u)
    k8 = 2.0 / (2.0 - u * u)
    scale = 1.0 / (center * (height * ROWS))

    eye = (
        lax.broadcasted_iota(jnp.int32, (F, F), 0) == lax.broadcasted_iota(jnp.int32, (F, F), 1)
    ).astype(F32)
    first = wide(GRAM, F) * scale + eye * (lower / center)
    part1 = split(first)
    second = k1 * (2.0 * first - dot3(part1, part1))
    advance(1, 2)
    part2 = split(second)
    fourth = k2 * (2.0 * second - dot3(part2, part2))
    advance(1, 2)
    part4 = split(fourth)
    s4[...] = fourth
    slab = s4[window(me * SLAB, SLAB), :]
    row = lax.broadcasted_iota(jnp.int32, (SLAB, F), 0) + me * SLAB
    column = lax.broadcasted_iota(jnp.int32, (SLAB, F), 1)
    unit = (row == column).astype(F32)
    eighth = k4 * (2.0 * slab - dot3(split(slab), part4))
    value = k8 * (2.0 * unit - eighth)
    value = k4 * (2.0 * value - dot3(split(value), part4))
    value = k2 * (2.0 * value - dot3(split(value), part2))
    value = k1 * (2.0 * value - dot3(split(value), part1))
    value = value * scale
    across = [[], []]

    def cross_planes(k, value):
        slabs[plane, k] = value
        mine = slabs.at[plane, k]
        for d in range(1, PLANES):
            copy = pltpu.make_async_remote_copy(
                src_ref=mine, dst_ref=mine, send_sem=plane_send.at[k, d], recv_sem=plane_recv.at[k, d],
                device_id={"cls": lax.rem(plane + d, PLANES)}, device_id_type=pl.DeviceIdType.MESH,
            )
            copy.start()
            across[k].append(copy)

    cross_planes(0, value)
    while not done[1]:
        advance(1, 2)
    cross_planes(1, dot3(split(value), split(wide(CROSS, F))))
    while not done[2]:
        advance(2)

    def moment(j):
        return split(wide(MOMENT + 2 * F * j, 2 * LANES))

    def product(z, k, right):
        return dot3(split(slabs[z, k]), right)

    def product2(z, k, right):
        high, low = split(slabs[z, k])
        return jnp.dot(high, right, preferred_element_type=F32) + jnp.dot(low, right, preferred_element_type=F32)

    def broadcast(j, w):
        w_out[j] = w
        mine = wh_out.at[j, pl.ds(pl.multiple_of(me * SLAB, SLAB), SLAB)]
        wh_out[j, pl.ds(pl.multiple_of(me * SLAB, SLAB), SLAB), :] = w.astype(BF)

        def tell(d, carry):
            pltpu.make_async_remote_copy(
                src_ref=mine, dst_ref=mine, send_sem=wide_send.at[j], recv_sem=wide_recv.at[j],
                device_id={"rows": lax.rem(me + d, ROWS)}, device_id_type=pl.DeviceIdType.MESH,
            ).start()
            return carry

        lax.fori_loop(1, ROWS, tell, 0)

    def all_but_one(j):
        part = wh_out.at[j, pl.ds(0, (ROWS - 1) * SLAB)]
        return pltpu.make_async_remote_copy(
            src_ref=part, dst_ref=part, send_sem=wide_send.at[j], recv_sem=wide_recv.at[j],
            device_id=place.partner, device_id_type=pl.DeviceIdType.MESH,
        )

    for copy in across[0]:
        copy.wait_recv()
    broadcast(0, product(0, 0, moment(0)))
    w1 = product(1, 0, moment(1))
    w2 = product(2, 0, moment(2))
    for copy in across[1]:
        copy.wait_recv()
    all_but_one(0).wait_recv()
    broadcast(1, w1 - product2(1, 1, wh_out[0]))
    w2 = w2 - product2(2, 1, wh_out[0])
    all_but_one(1).wait_recv()
    broadcast(2, w2 - product2(3, 1, wh_out[1]))
    all_but_one(2).wait_recv()
    for copy in copies + across[0] + across[1]:
        copy.wait_send()
    for j in range(NBLK):
        all_but_one(j).wait_send()
    for copy in stores:
        copy.wait()


def exchange_call(order, bounds, phases, data, projections, targets):
    vmem = pl.BlockSpec(memory_space=pltpu.VMEM)
    smem = pl.BlockSpec(memory_space=pltpu.SMEM)
    hbm = pl.BlockSpec(memory_space=pl.ANY)
    rows, classes = targets.shape
    buffers = []
    for _, height, direct in CHUNKS:
        buffers += [
            pltpu.VMEM((height // 2, LANES), F32),
            pltpu.VMEM((height // 2, LANES), F32),
            pltpu.VMEM(ring_shape(height // 16, direct[0]), F32),
            pltpu.VMEM(ring_shape(height // 64, direct[1]), F32),
            pltpu.VMEM((height // 8, LANES), F32),
        ]
    dma = pltpu.SemaphoreType.DMA
    return pl.pallas_call(
        functools.partial(exchange_kernel, sine_coefficients(math.sqrt(2.0 / F))),
        in_specs=[smem, smem, vmem, hbm, hbm, hbm],
        out_specs=[vmem, vmem, hbm],
        out_shape=[
            jax.ShapeDtypeStruct((NBLK, SLAB, classes), F32),
            jax.ShapeDtypeStruct((NBLK, F, classes), BF),
            jax.ShapeDtypeStruct((NBLK, rows, F), BF),
        ],
        scratch_shapes=[
            pltpu.VMEM(data.shape, BF),
            pltpu.VMEM(projections.shape, BF),
            pltpu.VMEM((data.shape[1], F), BF),
            pltpu.VMEM(targets.shape, BF),
            pltpu.VMEM((NBLK, rows, F), BF),
            pltpu.VMEM((HEIGHT, LANES), F32),
            pltpu.VMEM((HEIGHT, LANES), F32),
            pltpu.VMEM((F, F), F32),
            pltpu.VMEM((PLANES, 2, SLAB, F), F32),
            *buffers,
            dma((len(CHUNKS), COPIES)),
            dma((len(CHUNKS), COPIES)),
            dma((2, PLANES)),
            dma((2, PLANES)),
            dma((NBLK,)),
            dma((NBLK,)),
            dma((2 + TILES,)),
            dma((NBLK,)),
        ],
        compiler_params=pltpu.CompilerParams(collective_id=0, has_side_effects=True),
        name="exchange",
    )(order, bounds, phases.reshape(1, -1), data, projections, targets)


def residual_kernel(order, feats, half, targets, w, weights, residual):
    @pl.when(pl.program_id(0) == 0)
    def _():
        for turn in range(NBLK):
            weights[order[turn]] = w[turn]

    total = jnp.dot(feats[0], half[0], preferred_element_type=F32)
    for turn in range(1, NBLK):
        total = total + jnp.dot(feats[turn], half[turn], preferred_element_type=F32)
    residual[...] = targets[...].astype(F32) - total


def residual_call(order, feats, half, targets, w):
    rows, classes = targets.shape
    tile = RESIDUAL_TILE
    return pl.pallas_call(
        residual_kernel,
        grid_spec=pltpu.PrefetchScalarGridSpec(
            num_scalar_prefetch=1,
            grid=(rows // tile,),
            in_specs=[
                pl.BlockSpec((NBLK, tile, F), lambda i, n: (0, i, 0)),
                pl.BlockSpec((NBLK, F, classes), lambda i, n: (0, 0, 0)),
                pl.BlockSpec((tile, classes), lambda i, n: (i, 0)),
                pl.BlockSpec((NBLK, SLAB, classes), lambda i, n: (0, 0, 0)),
            ],
            out_specs=[
                pl.BlockSpec((NBLK, SLAB, classes), lambda i, n: (0, 0, 0)),
                pl.BlockSpec((tile, classes), lambda i, n: (i, 0)),
            ],
        ),
        out_shape=[
            jax.ShapeDtypeStruct((NBLK, SLAB, classes), F32),
            jax.ShapeDtypeStruct((rows, classes), F32),
        ],
        name="residual",
    )(order, feats, half, targets, w)


def body(data, projections, phases, targets, bounds, order):
    w, half, feats = exchange_call(order, bounds, phases, data, projections, targets)
    weights, residual = residual_call(order, feats, half, targets, w)
    return (weights, residual)


def solution(mesh):
    return jax.shard_map(
        body,
        mesh=mesh,
        in_specs=(P("rows", None), P(), P(), P("rows", "cls"), P(), P()),
        out_specs=(P(None, "rows", "cls"), P("rows", "cls")),
        check_vma=False,
    )
```

time: 127 us -> 94.9 us (0.75)
  Pallas kernels: 103 us -> 91.3 us
  between operations: 11.6 us -> 0.64 us
  matrix products: 6.12 us -> 0 us
  local copies, waits for them, and re-layouts: 4.64 us -> 2.63 us
    pallas_call x2, Pallas kernels: 103 us -> 91.3 us  [the longest x1 82.4 us: exchange_call(): pl.pallas_call(functools.partial(exchange_kernel, sine_coefficients(math....]
    dot_general x1 -> x0, matrix products: 6.12 us -> none  [body(): jnp.dot(feats, half, preferred_element_type=F32)]
    slice x2 -> x0, local copies, waits for them, and re-layouts: 1.98 us -> none  [the longest x1 1.46 us: body(): order[turn]]
where the time goes in v3:
time: 94.9 us; the launch traced here: 94.5 us
  Pallas kernels  91.3 us (96%)
  local copies, waits for them, and re-layouts  2.63 us (3%)
    pallas_call x1, Pallas kernels, exchange_call(): pl.pallas_call(functools.partial(exchange_kernel, sine_coefficients(math....  82.4 us
    pallas_call x1, Pallas kernels, residual_call(): pl.pallas_call(residual_kernel, grid_spec=pltpu.PrefetchScalarGridSpec(nu...  8.86 us

profile of v3, /device:TPU:1, one launch (start us, length us, event | category | flops | bytes accessed | tf_op | source)
XLA Modules:
  0.0 94.5 jit_solution(10560824434345660793)
XLA Ops:
  0.6 1.3 %copy.8.bounds = f32[3,2]{1,0:T(4,128)} copy(f32[3,2]{0,1:T(2,128)} %param.10) | data formatting | bytes 48 | tf_op args[4]
  2.0 1.3 %reshape.7.phases = f32[1,1536]{1,0:T(1,128)} reshape(f32[1536]{0:T(1024)} %param.8) | data formatting | bytes 12288 | tf_op jit(solution)/shard_map/reshape | solution.py:491
  3.3 82.4 %exchange.1 = (f32[3,16,256]{2,1,0:T(8,128)}, bf16[3,512,256]{2,1,0:T(8,128)(2,1)}, bf16[3,2048,512]{2,1,0:T(8,128)(2,1)}) custom-call(s32[3]{0:T(128)} %order.3, f32[3,2]{1,0:T(4,128)} %copy.8.bounds, f32[1,1536]{1,0:T(1,128)} %reshape.7.phases, bf16[2048,512]{1,0:T(8,128)(2,1)} %data_in.1, bf16[512,1536]{1,0:T(8,128)(2,1)} %proj_in.1, ...), custom_call_target="tpu_custom_call" | custom-call | tf_op jit(solution)/shard_map/exchange/pallas_call | solution.py:460
  85.7 8.9 %residual.1 = (f32[3,16,256]{2,1,0:T(8,128)}, f32[2048,256]{1,0:T(8,128)}) custom-call(s32[3]{0:T(128)} %order.3, bf16[3,2048,512]{2,1,0:T(8,128)(2,1)} %get-tuple-element.5.feats, bf16[3,512,256]{2,1,0:T(8,128)(2,1)} %get-tuple-element.6.half, bf16[2048,256]{1,0:T(8,128)(2,1)} %targets.1, f32[3,16,256]{2,1,0:T(8,128)} %get-tuple-element.7.w), custom_call_target="tpu_custom_call" | custom-call | tf_op jit(solution)/shard_map/residual/pallas_call | solution.py:509

commit v4 on v3

--- a/solution.py
+++ b/solution.py
@@ -11,7 +11,7 @@
 F = 512
 NBLK = 3
 TILE = 512
-RESIDUAL_TILE = 256
+RESIDUAL_TILE = 512
 TILES = 4
 SLAB = 16
 BF = jnp.bfloat16
@@ -19,7 +19,8 @@
 LANES = 128
 ROWS = 32
 PLANES = 4
-GRAM, CROSS, MOMENT, HEIGHT = 0, 4 * F, 8 * F, 14 * F
+GRAM, CROSS, MOMENT, HEIGHT = 0, 3 * F, 7 * F, 13 * F
+HALF = F // 2
 TURN = 1.0 / (2.0 * math.pi)
 
 
@@ -80,24 +81,14 @@
     return pl.ds(pl.multiple_of(start, 8), size)
 
 
-CHUNKS = (
-    (GRAM, 4 * F, (True, True, True, True)),
-    (CROSS, 4 * F, (True, True, True, True)),
-    (MOMENT, 6 * F, (False, True, True, False)),
-)
-COPIES = 51
-
-
-def ring_shape(size, direct):
-    return (2, 3, size, LANES) if direct else (4, 4, size // 2, LANES)
+CHUNKS = ((GRAM, 3 * F), (CROSS, 4 * F), (MOMENT, 2 * F), (MOMENT + 2 * F, 4 * F))
+COPIES = 27
 
 
 def reduce_chunk(place, q, v, out, r0, acc, ring1, ring2, part1, send_sem, recv_sem, copies):
-    base, height, direct = CHUNKS[q]
+    base, height = CHUNKS[q]
     half = height // 2
-    ways = [(part, h) for part in range(2) for h in range(2)]
-    hops = [(part, d) for part in range(2) for d in range(1, 4)]
-    sign = (1, -1)
+    hops = [(part, d) for d in (2, 1, 3) for part in range(2)]
 
     def send(k, source, target, device):
         copy = pltpu.make_async_remote_copy(
@@ -113,9 +104,9 @@
     first.wait_recv()
     acc[...] = v[window(base + place.core * half, half), :] + r0[...]
 
-    def scatter_direct(k, axes, source, origin, size, ring, store):
+    def scatter(k, axes, source, origin, size, ring, store):
         flights = {}
-        for part, d in sorted(hops, key=lambda hop: hop[1] != 2):
+        for part, d in hops:
             target = mod4(place.at(axes[part]) + d)
             piece = source.at[window(origin(part) + target * size, size)]
             flights[part, d] = send(k + part * 3 + d - 1, piece, ring.at[part, d - 1], place.near(axes[part], d))
@@ -125,108 +116,46 @@
             for d in range(1, 4):
                 flights[part, d].wait_recv()
                 total = total + ring[part, d - 1]
-            store(part, 0, total)
-
-    def gather_direct(k, axes, origin, size):
+            store(part, total)
+
+    def gather(k, axes, origin, size):
         flights = []
-        for part, d in sorted(hops, key=lambda hop: hop[1] != 2):
+        for part, d in hops:
             mine = out.at[window(base + origin(part) + place.at(axes[part]) * size, size)]
             flights.append(send(k + part * 3 + d - 1, mine, mine, place.near(axes[part], d)))
         yield
         for copy in flights:
             copy.wait_recv()
 
-    def scatter_ring(k, axes, source, origin, size, ring, store):
-        small = size // 2
-
-        def piece(part, i, h):
-            return window(origin(part) + i * size + h * small, small)
-
-        far, close, on = {}, {}, {}
-        for part, h in ways:
-            axis, s = axes[part], sign[h]
-            i = place.at(axis)
-            n = part * 2 + h
-            far[n] = send(k + n, source.at[piece(part, mod4(i + 2), h)], ring.at[n, 0], place.near(axis, s))
-            close[n] = send(k + 4 + n, source.at[piece(part, mod4(i - s), h)], ring.at[n, 1], place.near(axis, -s))
-        yield
-        for part, h in ways:
-            axis, s = axes[part], sign[h]
-            i = place.at(axis)
-            n = part * 2 + h
-            far[n].wait_recv()
-            ring[n, 3] = source[piece(part, mod4(i + s), h), :] + ring[n, 0]
-            on[n] = send(k + 8 + n, ring.at[n, 3], ring.at[n, 2], place.near(axis, s))
-        yield
-        for part, h in ways:
-            i = place.at(axes[part])
-            n = part * 2 + h
-            close[n].wait_recv()
-            on[n].wait_recv()
-            store(part, h, source[piece(part, i, h), :] + ring[n, 1] + ring[n, 2])
-
-    def gather_ring(k, axes, origin, size):
-        small = size // 2
-
-        def piece(part, i, h):
-            return out.at[window(base + origin(part) + i * size + h * small, small)]
-
-        ahead, back, on = {}, {}, {}
-        for part, h in ways:
-            axis, s = axes[part], sign[h]
-            n = part * 2 + h
-            mine = piece(part, place.at(axis), h)
-            ahead[n] = send(k + n, mine, mine, place.near(axis, s))
-            back[n] = send(k + 4 + n, mine, mine, place.near(axis, -s))
-        yield
-        for part, h in ways:
-            axis, s = axes[part], sign[h]
-            n = part * 2 + h
-            ahead[n].wait_recv()
-            theirs = piece(part, mod4(place.at(axis) - s), h)
-            on[n] = send(k + 8 + n, theirs, theirs, place.near(axis, s))
-        yield
-        for n in range(4):
-            back[n].wait_recv()
-            on[n].wait_recv()
-
-    def pick(straight, ringed, stage):
-        return straight if direct[stage] else ringed
-
     one, two = ("x", "y"), ("y", "x")
     quarter, sixteenth, last = height // 4, height // 16, height // 64
 
-    def store1(part, h, value):
-        start = part * sixteenth + h * value.shape[0]
-        part1[start:start + value.shape[0], :] = value
-
-    scatter = pick(scatter_direct, scatter_ring, 0)
+    def store1(part, value):
+        part1[part * sixteenth:(part + 1) * sixteenth, :] = value
+
     yield from scatter(1, one, acc, lambda part: part * quarter, sixteenth, ring1, store1)
 
     def own(part):
         return place.core * half + part * quarter + place.at(one[part]) * sixteenth
 
-    def store2(part, h, value):
-        start = base + own(part) + place.at(two[part]) * last + h * value.shape[0]
-        out[window(start, value.shape[0]), :] = value
-
-    scatter = pick(scatter_direct, scatter_ring, 1)
-    yield from scatter(13, two, part1, lambda part: part * sixteenth, last, ring2, store2)
-    yield from pick(gather_direct, gather_ring, 2)(25, two, own, last)
-    gather = pick(gather_direct, gather_ring, 3)
-    yield from gather(37, one, lambda part: place.core * half + part * quarter, sixteenth)
+    def store2(part, value):
+        out[window(base + own(part) + place.at(two[part]) * last, last), :] = value
+
+    yield from scatter(7, two, part1, lambda part: part * sixteenth, last, ring2, store2)
+    yield from gather(13, two, own, last)
+    yield from gather(19, one, lambda part: place.core * half + part * quarter, sixteenth)
     finals = []
     for part in range(2):
         mine = out.at[window(base + place.core * half + part * quarter, quarter)]
-        finals.append(send(49 + part, mine, mine, place.partner))
+        finals.append(send(25 + part, mine, mine, place.partner))
     yield
     for copy in finals:
         copy.wait_recv()
 
 
 def exchange_kernel(
-    coefficients, order, bounds, phases, data_in, proj_in, targets_in, w_out, wh_out, feats_out,
-    data, proj, chosen, targets, feats, v, out, s4, slabs, *scratch
+    coefficients, order, bounds, phases, data_in, proj_in, targets_in, w_out, wh_out, feats_out, left_out,
+    data, proj, chosen, targets, feats, left, v, out, s4, slabs, *scratch
 ):
     place = Place()
     buffers = scratch[:5 * len(CHUNKS)]
@@ -286,7 +215,7 @@
         chosen[...] = pick(turn, columns(proj))
 
     def features(turn, tiles):
-        shift = pick(turn, columns(phases)) * TURN
+        shift = pick(turn, [phases[j * F:(j + 1) * F] for j in range(NBLK)])[None, :] * TURN
         for t in tiles:
             rows = pl.ds(t * TILE, TILE)
             angle = jnp.dot(data[rows, :], chosen[...], preferred_element_type=F32)
@@ -297,46 +226,48 @@
         for k in range(width // LANES):
             v[window(base + k * tall, tall), :] = value[:, k * LANES:(k + 1) * LANES]
 
-    def keep(n, turn):
-        copy = pltpu.make_async_copy(feats.at[turn], feats_out.at[turn], store_sem.at[n])
-        copy.start()
-        return copy
-
     def moments(turn):
         put(MOMENT + 2 * F * turn, lax.dot_general(feats[turn], targets[...], contract, preferred_element_type=F32))
 
+    def gram():
+        for n in range(2):
+            lhs = feats[turn_a, :, n * HALF:(n + 1) * HALF]
+            rhs = feats[turn_a, :, n * HALF:]
+            put(GRAM + n * 2 * F, lax.dot_general(lhs, rhs, contract, preferred_element_type=F32))
+
+    G, C, M, N = range(4)
     loads[0].wait()
+    choose(turn_a)
     for t in range(TILES):
         loads[1 + t].wait()
-    choose(turn_a)
-    features(turn_a, range(TILES))
-    put(GRAM, lax.dot_general(feats[turn_a], feats[turn_a], contract, preferred_element_type=F32))
+        features(turn_a, [t])
+    gram()
     pl.semaphore_wait(barrier, ROWS - 1 + PLANES - 1)
-    advance(0)
+    advance(G)
     choose(turn_b)
     features(turn_b, range(2))
-    advance(0)
+    advance(G)
     features(turn_b, range(2, TILES))
     put(CROSS, lax.dot_general(feats[turn_a], feats[turn_b], contract, preferred_element_type=F32))
-    advance(0, 1)
+    advance(C)
     choose(turn_c)
-    features(turn_c, range(2))
-    advance(0, 1)
-    features(turn_c, range(2, TILES))
-    advance(0)
+    features(turn_c, range(3))
+    advance(G, C)
+    features(turn_c, range(3, TILES))
     loads[1 + TILES].wait()
-    for turn in (turn_a, turn_b, turn_c):
-        moments(turn)
-    advance(0, 1, 2)
-    stores = [keep(n, turn) for n, turn in enumerate((turn_a, turn_b, turn_c))]
-    while not done[0]:
-        advance(0, 1, 2)
-
-    def wide(base, width):
-        return jnp.concatenate([out[window(base + k * F, F), :] for k in range(width // LANES)], axis=1)
-
-    lower = jnp.full((1, F), pick(turn_a, [bounds[j, 0] for j in range(NBLK)]), F32)
-    upper = jnp.full((1, F), pick(turn_a, [bounds[j, 1] for j in range(NBLK)]), F32)
+    moments(0)
+    advance(M)
+    moments(1)
+    moments(2)
+    keep = pltpu.make_async_copy(feats.at[NBLK - 1], feats_out, store_sem.at[0])
+    keep.start()
+    advance(G, N, M, N, C, G, M, N, C, G, M, N, C, G)
+
+    def wide(base, width, tall=F):
+        return jnp.concatenate([out[window(base + k * tall, tall), :] for k in range(width // LANES)], axis=1)
+
+    lower = jnp.full((1, F), pick(turn_a, [bounds[0, j] for j in range(NBLK)]), F32)
+    upper = jnp.full((1, F), pick(turn_a, [bounds[1, j] for j in range(NBLK)]), F32)
     center = 0.5 * (upper + lower)
     u = 0.5 * (upper - lower) / center
     k1 = 2.0 / (2.0 - u * u)
@@ -351,13 +282,15 @@
     eye = (
         lax.broadcasted_iota(jnp.int32, (F, F), 0) == lax.broadcasted_iota(jnp.int32, (F, F), 1)
     ).astype(F32)
-    first = wide(GRAM, F) * scale + eye * (lower / center)
+    top = wide(GRAM, F, HALF)
+    corner = wide(GRAM + 2 * F, HALF, HALF)
+    whole = jnp.concatenate([top, jnp.concatenate([top[:, HALF:].T, corner], axis=1)], axis=0)
+    first = whole * scale + eye * (lower / center)
     part1 = split(first)
     second = k1 * (2.0 * first - dot3(part1, part1))
-    advance(1, 2)
     part2 = split(second)
     fourth = k2 * (2.0 * second - dot3(part2, part2))
-    advance(1, 2)
+    advance(M, N)
     part4 = split(fourth)
     s4[...] = fourth
     slab = s4[window(me * SLAB, SLAB), :]
@@ -384,11 +317,9 @@
             across[k].append(copy)
 
     cross_planes(0, value)
-    while not done[1]:
-        advance(1, 2)
+    advance(C, M, C)
     cross_planes(1, dot3(split(value), split(wide(CROSS, F))))
-    while not done[2]:
-        advance(2)
+    advance(M)
 
     def moment(j):
         return split(wide(MOMENT + 2 * F * j, 2 * LANES))
@@ -421,9 +352,17 @@
             device_id=place.partner, device_id_type=pl.DeviceIdType.MESH,
         )
 
+    def subtract(turn, start):
+        for t in range(TILES):
+            rows = pl.ds(t * TILE, TILE)
+            before = targets[rows, :].astype(F32) if start else left[rows, :]
+            left[rows, :] = before - jnp.dot(feats[turn, rows, :], wh_out[turn], preferred_element_type=F32)
+
     for copy in across[0]:
         copy.wait_recv()
     broadcast(0, product(0, 0, moment(0)))
+    advance(N, N)
+    assert all(done)
     w1 = product(1, 0, moment(1))
     w2 = product(2, 0, moment(2))
     for copy in across[1]:
@@ -431,15 +370,19 @@
     all_but_one(0).wait_recv()
     broadcast(1, w1 - product2(1, 1, wh_out[0]))
     w2 = w2 - product2(2, 1, wh_out[0])
+    subtract(0, True)
     all_but_one(1).wait_recv()
     broadcast(2, w2 - product2(3, 1, wh_out[1]))
+    subtract(1, False)
+    hand = pltpu.make_async_copy(left, left_out, store_sem.at[1])
+    hand.start()
     all_but_one(2).wait_recv()
     for copy in copies + across[0] + across[1]:
         copy.wait_send()
     for j in range(NBLK):
         all_but_one(j).wait_send()
-    for copy in stores:
-        copy.wait()
+    keep.wait()
+    hand.wait()
 
 
 def exchange_call(order, bounds, phases, data, projections, targets):
@@ -448,23 +391,24 @@
     hbm = pl.BlockSpec(memory_space=pl.ANY)
     rows, classes = targets.shape
     buffers = []
-    for _, height, direct in CHUNKS:
+    for _, height in CHUNKS:
         buffers += [
             pltpu.VMEM((height // 2, LANES), F32),
             pltpu.VMEM((height // 2, LANES), F32),
-            pltpu.VMEM(ring_shape(height // 16, direct[0]), F32),
-            pltpu.VMEM(ring_shape(height // 64, direct[1]), F32),
+            pltpu.VMEM((2, 3, height // 16, LANES), F32),
+            pltpu.VMEM((2, 3, height // 64, LANES), F32),
             pltpu.VMEM((height // 8, LANES), F32),
         ]
     dma = pltpu.SemaphoreType.DMA
     return pl.pallas_call(
         functools.partial(exchange_kernel, sine_coefficients(math.sqrt(2.0 / F))),
         in_specs=[smem, smem, vmem, hbm, hbm, hbm],
-        out_specs=[vmem, vmem, hbm],
+        out_specs=[vmem, vmem, hbm, hbm],
         out_shape=[
             jax.ShapeDtypeStruct((NBLK, SLAB, classes), F32),
             jax.ShapeDtypeStruct((NBLK, F, classes), BF),
-            jax.ShapeDtypeStruct((NBLK, rows, F), BF),
+            jax.ShapeDtypeStruct((rows, F), BF),
+            jax.ShapeDtypeStruct((rows, classes), F32),
         ],
         scratch_shapes=[
             pltpu.VMEM(data.shape, BF),
@@ -472,6 +416,7 @@
             pltpu.VMEM((data.shape[1], F), BF),
             pltpu.VMEM(targets.shape, BF),
             pltpu.VMEM((NBLK, rows, F), BF),
+            pltpu.VMEM((rows, classes), F32),
             pltpu.VMEM((HEIGHT, LANES), F32),
             pltpu.VMEM((HEIGHT, LANES), F32),
             pltpu.VMEM((F, F), F32),
@@ -484,27 +429,24 @@
             dma((NBLK,)),
             dma((NBLK,)),
             dma((2 + TILES,)),
-            dma((NBLK,)),
+            dma((2,)),
         ],
         compiler_params=pltpu.CompilerParams(collective_id=0, has_side_effects=True),
         name="exchange",
-    )(order, bounds, phases.reshape(1, -1), data, projections, targets)
-
-
-def residual_kernel(order, feats, half, targets, w, weights, residual):
+    )(order, bounds.T, phases, data, projections, targets)
+
+
+def residual_kernel(order, feats, half, left, w, weights, residual):
     @pl.when(pl.program_id(0) == 0)
     def _():
         for turn in range(NBLK):
             weights[order[turn]] = w[turn]
 
-    total = jnp.dot(feats[0], half[0], preferred_element_type=F32)
-    for turn in range(1, NBLK):
-        total = total + jnp.dot(feats[turn], half[turn], preferred_element_type=F32)
-    residual[...] = targets[...].astype(F32) - total
-
-
-def residual_call(order, feats, half, targets, w):
-    rows, classes = targets.shape
+    residual[...] = left[...] - jnp.dot(feats[...], half[0], preferred_element_type=F32)
+
+
+def residual_call(order, feats, half, left, w):
+    rows, classes = left.shape
     tile = RESIDUAL_TILE
     return pl.pallas_call(
         residual_kernel,
@@ -512,8 +454,8 @@
             num_scalar_prefetch=1,
             grid=(rows // tile,),
             in_specs=[
-                pl.BlockSpec((NBLK, tile, F), lambda i, n: (0, i, 0)),
-                pl.BlockSpec((NBLK, F, classes), lambda i, n: (0, 0, 0)),
+                pl.BlockSpec((tile, F), lambda i, n: (i, 0)),
+                pl.BlockSpec((1, F, classes), lambda i, n: (NBLK - 1, 0, 0)),
                 pl.BlockSpec((tile, classes), lambda i, n: (i, 0)),
                 pl.BlockSpec((NBLK, SLAB, classes), lambda i, n: (0, 0, 0)),
             ],
@@ -527,12 +469,12 @@
             jax.ShapeDtypeStruct((rows, classes), F32),
         ],
         name="residual",
-    )(order, feats, half, targets, w)
+    )(order, feats, half, left, w)
 
 
 def body(data, projections, phases, targets, bounds, order):
-    w, half, feats = exchange_call(order, bounds, phases, data, projections, targets)
-    weights, residual = residual_call(order, feats, half, targets, w)
+    w, half, feats, left = exchange_call(order, bounds, phases, data, projections, targets)
+    weights, residual = residual_call(order, feats, half, left, w)
     return (weights, residual)
 
 

time: 94.9 us -> 72.1 us (0.76)
  Pallas kernels: 91.3 us -> 71.2 us
  local copies, waits for them, and re-layouts: 2.63 us -> 0 us
    pallas_call x1, Pallas kernels: 82.4 us -> 65.8 us  [exchange_call(): pl.pallas_call(functools.partial(exchange_kernel, sine_coefficients(math....]
    pallas_call x1, Pallas kernels: 8.86 us -> 5.42 us  [residual_call(): pl.pallas_call(residual_kernel, grid_spec=pltpu.PrefetchScalarGridSpec(nu...]
    unnamed x1 -> x0, local copies, waits for them, and re-layouts: 1.34 us -> none
    reshape x1 -> x0, local copies, waits for them, and re-layouts: 1.29 us -> none  [exchange_call(): phases.reshape(1, -1)]
where the time goes in v4:
time: 72.1 us; the launch traced here: 71.8 us
  Pallas kernels  71.2 us (99%)
    pallas_call x1, Pallas kernels, exchange_call(): pl.pallas_call(functools.partial(exchange_kernel, sine_coefficients(math....  65.8 us
    pallas_call x1, Pallas kernels, residual_call(): pl.pallas_call(residual_kernel, grid_spec=pltpu.PrefetchScalarGridSpec(nu...  5.42 us

profile of v4, /device:TPU:1, one launch (start us, length us, event | category | flops | bytes accessed | tf_op | source)
XLA Modules:
  0.0 71.8 jit_solution(5290488766986742143)
XLA Ops:
  0.6 65.8 %exchange.1 = (f32[3,16,256]{2,1,0:T(8,128)}, bf16[3,512,256]{2,1,0:T(8,128)(2,1)}, bf16[2048,512]{1,0:T(8,128)(2,1)}, f32[2048,256]{1,0:T(8,128)}) custom-call(s32[3]{0:T(128)} %order.3, f32[2,3]{1,0:T(2,128)} %bitcast.1, f32[1536]{0:T(1024)} %phases.1, bf16[2048,512]{1,0:T(8,128)(2,1)} %data_in.1, bf16[512,1536]{1,0:T(8,128)(2,1)} %proj_in.1, ...), custom_call_target="tpu_custom_call" | custom-call | tf_op jit(solution)/shard_map/exchange/pallas_call | solution.py:403
  66.4 5.4 %residual.1 = (f32[3,16,256]{2,1,0:T(8,128)}, f32[2048,256]{1,0:T(8,128)}) custom-call(s32[3]{0:T(128)} %order.3, bf16[2048,512]{1,0:T(8,128)(2,1)} %get-tuple-element.6.feats, bf16[3,512,256]{2,1,0:T(8,128)(2,1)} %get-tuple-element.7.half, f32[2048,256]{1,0:T(8,128)} %get-tuple-element.8.left, f32[3,16,256]{2,1,0:T(8,128)} %get-tuple-element.9.w), custom_call_target="tpu_custom_call" | custom-call | tf_op jit(solution)/shard_map/residual/pallas_call | solution.py:451

commit v5 on v4

--- a/solution.py
+++ b/solution.py
@@ -155,7 +155,7 @@
 
 def exchange_kernel(
     coefficients, order, bounds, phases, data_in, proj_in, targets_in, w_out, wh_out, feats_out, left_out,
-    data, proj, chosen, targets, feats, left, v, out, s4, slabs, *scratch
+    data, proj, chosen, targets, feats, left, v, out, s1, slabs, *scratch
 ):
     place = Place()
     buffers = scratch[:5 * len(CHUNKS)]
@@ -172,17 +172,11 @@
 
     barrier = pltpu.get_barrier_semaphore()
 
-    def greet(d, carry):
-        pl.semaphore_signal(
-            barrier, inc=1, device_id={"rows": lax.rem(me + d, ROWS)}, device_id_type=pl.DeviceIdType.MESH
-        )
-        return carry
-
-    lax.fori_loop(1, ROWS, greet, 0)
-    for d in range(1, PLANES):
-        pl.semaphore_signal(
-            barrier, inc=1, device_id={"cls": lax.rem(plane + d, PLANES)}, device_id_type=pl.DeviceIdType.MESH
-        )
+    greeted = [place.partner]
+    greeted += [place.near(axis, d) for axis in ("x", "y") for d in range(1, 4)]
+    greeted += [{"cls": lax.rem(plane + d, PLANES)} for d in range(1, PLANES)]
+    for device in greeted:
+        pl.semaphore_signal(barrier, inc=1, device_id=device, device_id_type=pl.DeviceIdType.MESH)
 
     copies = []
     runs = [
@@ -200,8 +194,9 @@
                     done[q] = True
 
     turn_a = jnp.minimum(plane, 2)
-    turn_b = jnp.where(plane == 0, 1, jnp.where(plane == 3, 1, 0))
+    turn_b = jnp.where(plane == 0, 1, 0)
     turn_c = 3 - turn_a - turn_b
+    turn_x = jnp.where(plane == 3, 1, 0)
     contract = (((0,), (0,)), ((), ()))
 
     def pick(turn, values):
@@ -242,26 +237,26 @@
         loads[1 + t].wait()
         features(turn_a, [t])
     gram()
-    pl.semaphore_wait(barrier, ROWS - 1 + PLANES - 1)
+    pl.semaphore_wait(barrier, len(greeted))
     advance(G)
     choose(turn_b)
-    features(turn_b, range(2))
+    features(turn_b, range(3))
     advance(G)
-    features(turn_b, range(2, TILES))
-    put(CROSS, lax.dot_general(feats[turn_a], feats[turn_b], contract, preferred_element_type=F32))
-    advance(C)
-    choose(turn_c)
-    features(turn_c, range(3))
-    advance(G, C)
-    features(turn_c, range(3, TILES))
+    features(turn_b, range(3, TILES))
     loads[1 + TILES].wait()
     moments(0)
+    choose(turn_c)
+    features(turn_c, range(2))
     advance(M)
+    features(turn_c, range(2, TILES))
+    advance(G)
+    put(CROSS, lax.dot_general(feats[turn_a], feats[turn_x], contract, preferred_element_type=F32))
+    advance(C, M)
     moments(1)
     moments(2)
     keep = pltpu.make_async_copy(feats.at[NBLK - 1], feats_out, store_sem.at[0])
     keep.start()
-    advance(G, N, M, N, C, G, M, N, C, G, M, N, C, G)
+    advance(G, C, N, M, N, G, C, M, N, G, C, M, N, C, G)
 
     def wide(base, width, tall=F):
         return jnp.concatenate([out[window(base + k * tall, tall), :] for k in range(width // LANES)], axis=1)
@@ -286,40 +281,48 @@
     corner = wide(GRAM + 2 * F, HALF, HALF)
     whole = jnp.concatenate([top, jnp.concatenate([top[:, HALF:].T, corner], axis=1)], axis=0)
     first = whole * scale + eye * (lower / center)
-    part1 = split(first)
-    second = k1 * (2.0 * first - dot3(part1, part1))
-    part2 = split(second)
-    fourth = k2 * (2.0 * second - dot3(part2, part2))
-    advance(M, N)
-    part4 = split(fourth)
-    s4[...] = fourth
-    slab = s4[window(me * SLAB, SLAB), :]
+    s1[...] = first
     row = lax.broadcasted_iota(jnp.int32, (SLAB, F), 0) + me * SLAB
     column = lax.broadcasted_iota(jnp.int32, (SLAB, F), 1)
     unit = (row == column).astype(F32)
-    eighth = k4 * (2.0 * slab - dot3(split(slab), part4))
-    value = k8 * (2.0 * unit - eighth)
+    value = k1 * (2.0 * unit - s1[window(me * SLAB, SLAB), :])
+    part1 = split(first)
+    second = k1 * (2.0 * first - dot3(part1, part1))
+    advance(M)
+    part2 = split(second)
+    value = k2 * (2.0 * value - dot3(split(value), part2))
+    fourth = k2 * (2.0 * second - dot3(part2, part2))
+    advance(N)
+    part4 = split(fourth)
     value = k4 * (2.0 * value - dot3(split(value), part4))
-    value = k2 * (2.0 * value - dot3(split(value), part2))
-    value = k1 * (2.0 * value - dot3(split(value), part1))
+    once = dot3(split(value), part4)
+    value = k8 * (2.0 * value - k4 * (2.0 * once - dot3(split(once), part4)))
     value = value * scale
-    across = [[], []]
+    sends = (plane != PLANES - 1, plane != 0)
+
+    def slab_copy(k, source, d):
+        return pltpu.make_async_remote_copy(
+            src_ref=slabs.at[source, k], dst_ref=slabs.at[source, k],
+            send_sem=plane_send.at[k, d], recv_sem=plane_recv.at[k, source],
+            device_id={"cls": lax.rem(plane + d, PLANES)}, device_id_type=pl.DeviceIdType.MESH,
+        )
 
     def cross_planes(k, value):
         slabs[plane, k] = value
-        mine = slabs.at[plane, k]
-        for d in range(1, PLANES):
-            copy = pltpu.make_async_remote_copy(
-                src_ref=mine, dst_ref=mine, send_sem=plane_send.at[k, d], recv_sem=plane_recv.at[k, d],
-                device_id={"cls": lax.rem(plane + d, PLANES)}, device_id_type=pl.DeviceIdType.MESH,
-            )
-            copy.start()
-            across[k].append(copy)
+
+        @pl.when(sends[k])
+        def _():
+            for d in (2, 1, 3):
+                slab_copy(k, plane, d).start()
+
+    def arrived(k, source):
+        @pl.when(plane != source)
+        def _():
+            slab_copy(k, source, 1).wait_recv()
 
     cross_planes(0, value)
-    advance(C, M, C)
+    advance(M, C, C)
     cross_planes(1, dot3(split(value), split(wide(CROSS, F))))
-    advance(M)
 
     def moment(j):
         return split(wide(MOMENT + 2 * F * j, 2 * LANES))
@@ -358,15 +361,16 @@
             before = targets[rows, :].astype(F32) if start else left[rows, :]
             left[rows, :] = before - jnp.dot(feats[turn, rows, :], wh_out[turn], preferred_element_type=F32)
 
-    for copy in across[0]:
-        copy.wait_recv()
+    arrived(0, 0)
     broadcast(0, product(0, 0, moment(0)))
     advance(N, N)
     assert all(done)
+    arrived(0, 1)
     w1 = product(1, 0, moment(1))
+    arrived(0, 2)
     w2 = product(2, 0, moment(2))
-    for copy in across[1]:
-        copy.wait_recv()
+    for source in range(1, PLANES):
+        arrived(1, source)
     all_but_one(0).wait_recv()
     broadcast(1, w1 - product2(1, 1, wh_out[0]))
     w2 = w2 - product2(2, 1, wh_out[0])
@@ -377,8 +381,14 @@
     hand = pltpu.make_async_copy(left, left_out, store_sem.at[1])
     hand.start()
     all_but_one(2).wait_recv()
-    for copy in copies + across[0] + across[1]:
+    for copy in copies:
         copy.wait_send()
+    for k in range(2):
+        @pl.when(sends[k])
+        def _():
+            for d in range(1, PLANES):
+                slab_copy(k, plane, d).wait_send()
+
     for j in range(NBLK):
         all_but_one(j).wait_send()
     keep.wait()
@@ -436,40 +446,57 @@
     )(order, bounds.T, phases, data, projections, targets)
 
 
-def residual_kernel(order, feats, half, left, w, weights, residual):
-    @pl.when(pl.program_id(0) == 0)
-    def _():
-        for turn in range(NBLK):
-            weights[order[turn]] = w[turn]
-
-    residual[...] = left[...] - jnp.dot(feats[...], half[0], preferred_element_type=F32)
+def residual_kernel(order, w, feats_in, half_in, left_in, weights, residual, feats, half, left, result, load_sem, store_sem):
+    tiles = left.shape[0] // RESIDUAL_TILE
+
+    def rows(t):
+        return pl.ds(t * RESIDUAL_TILE, RESIDUAL_TILE)
+
+    loads = [pltpu.make_async_copy(half_in.at[NBLK - 1], half, load_sem.at[2 * tiles])]
+    for t in range(tiles):
+        loads.append(pltpu.make_async_copy(feats_in.at[rows(t)], feats.at[rows(t)], load_sem.at[2 * t]))
+        loads.append(pltpu.make_async_copy(left_in.at[rows(t)], left.at[rows(t)], load_sem.at[2 * t + 1]))
+    for copy in loads:
+        copy.start()
+    for turn in range(NBLK):
+        weights[order[turn]] = w[turn]
+    loads[0].wait()
+    stores = []
+    for t in range(tiles):
+        loads[1 + 2 * t].wait()
+        loads[2 + 2 * t].wait()
+        product = jnp.dot(feats[rows(t), :], half[...], preferred_element_type=F32)
+        result[rows(t), :] = left[rows(t), :] - product
+        copy = pltpu.make_async_copy(result.at[rows(t)], residual.at[rows(t)], store_sem.at[t])
+        copy.start()
+        stores.append(copy)
+    for copy in stores:
+        copy.wait()
 
 
 def residual_call(order, feats, half, left, w):
     rows, classes = left.shape
-    tile = RESIDUAL_TILE
+    vmem = pl.BlockSpec(memory_space=pltpu.VMEM)
+    hbm = pl.BlockSpec(memory_space=pl.ANY)
+    tiles = rows // RESIDUAL_TILE
     return pl.pallas_call(
         residual_kernel,
-        grid_spec=pltpu.PrefetchScalarGridSpec(
-            num_scalar_prefetch=1,
-            grid=(rows // tile,),
-            in_specs=[
-                pl.BlockSpec((tile, F), lambda i, n: (i, 0)),
-                pl.BlockSpec((1, F, classes), lambda i, n: (NBLK - 1, 0, 0)),
-                pl.BlockSpec((tile, classes), lambda i, n: (i, 0)),
-                pl.BlockSpec((NBLK, SLAB, classes), lambda i, n: (0, 0, 0)),
-            ],
-            out_specs=[
-                pl.BlockSpec((NBLK, SLAB, classes), lambda i, n: (0, 0, 0)),
-                pl.BlockSpec((tile, classes), lambda i, n: (i, 0)),
-            ],
-        ),
+        in_specs=[pl.BlockSpec(memory_space=pltpu.SMEM), vmem, hbm, hbm, hbm],
+        out_specs=[vmem, hbm],
         out_shape=[
             jax.ShapeDtypeStruct((NBLK, SLAB, classes), F32),
             jax.ShapeDtypeStruct((rows, classes), F32),
         ],
+        scratch_shapes=[
+            pltpu.VMEM((rows, F), BF),
+            pltpu.VMEM((F, classes), BF),
+            pltpu.VMEM((rows, classes), F32),
+            pltpu.VMEM((rows, classes), F32),
+            pltpu.SemaphoreType.DMA((2 * tiles + 1,)),
+            pltpu.SemaphoreType.DMA((tiles,)),
+        ],
         name="residual",
-    )(order, feats, half, left, w)
+    )(order, w, feats, half, left)
 
 
 def body(data, projections, phases, targets, bounds, order):

time: 72.1 us -> 70.4 us (0.976)
  Pallas kernels: 71.2 us -> 69.4 us
    pallas_call x1, Pallas kernels: 65.8 us -> 64.1 us  [exchange_call(): pl.pallas_call(functools.partial(exchange_kernel, sine_coefficients(math....]
where the time goes in v5:
time: 70.4 us; the launch traced here: 70.2 us
  Pallas kernels  69.4 us (99%)
  between operations  0.8 us (1%)
    pallas_call x1, Pallas kernels, exchange_call(): pl.pallas_call(functools.partial(exchange_kernel, sine_coefficients(math....  64.1 us
    pallas_call x1, Pallas kernels, residual_call(): pl.pallas_call(residual_kernel, in_specs=[pl.BlockSpec(memory_space=pltpu...  5.31 us

profile of v5, /device:TPU:1, one launch (start us, length us, event | category | flops | bytes accessed | tf_op | source)
XLA Modules:
  0.0 70.2 jit_solution(10182360610631071091)
XLA Ops:
  0.6 64.1 %exchange.1 = (f32[3,16,256]{2,1,0:T(8,128)}, bf16[3,512,256]{2,1,0:T(8,128)(2,1)}, bf16[2048,512]{1,0:T(8,128)(2,1)}, f32[2048,256]{1,0:T(8,128)}) custom-call(s32[3]{0:T(128)} %order.3, f32[2,3]{1,0:T(2,128)} %bitcast.1, f32[1536]{0:T(1024)} %phases.1, bf16[2048,512]{1,0:T(8,128)(2,1)} %data_in.1, bf16[512,1536]{1,0:T(8,128)(2,1)} %proj_in.1, ...), custom_call_target="tpu_custom_call" | custom-call | tf_op jit(solution)/shard_map/exchange/pallas_call | solution.py:413
  64.8 5.3 %residual.1 = (f32[3,16,256]{2,1,0:T(8,128)}, f32[2048,256]{1,0:T(8,128)}) custom-call(s32[3]{0:T(128)} %order.3, f32[3,16,256]{2,1,0:T(8,128)} %get-tuple-element.6.w, bf16[2048,512]{1,0:T(8,128)(2,1)} %get-tuple-element.7.feats_in, bf16[3,512,256]{2,1,0:T(8,128)(2,1)} %get-tuple-element.8.half_in, f32[2048,256]{1,0:T(8,128)} %get-tuple-element.9.left_in), custom_call_target="tpu_custom_call" | custom-call | tf_op jit(solution)/shard_map/residual/pallas_call | solution.py:482

commit v6 on v5

--- a/solution.py
+++ b/solution.py
@@ -81,12 +81,18 @@
     return pl.ds(pl.multiple_of(start, 8), size)
 
 
-CHUNKS = ((GRAM, 3 * F), (CROSS, 4 * F), (MOMENT, 2 * F), (MOMENT + 2 * F, 4 * F))
+CHUNKS = (
+    (GRAM, 3 * F, True),
+    (CROSS, 4 * F, True),
+    *((MOMENT + 2 * F * j, 2 * F, False) for j in range(NBLK)),
+)
+CHIP_SLAB = 2 * SLAB
+CHIPS = ROWS // 2
 COPIES = 27
 
 
 def reduce_chunk(place, q, v, out, r0, acc, ring1, ring2, part1, send_sem, recv_sem, copies):
-    base, height = CHUNKS[q]
+    base, height, join = CHUNKS[q]
     half = height // 2
     hops = [(part, d) for d in (2, 1, 3) for part in range(2)]
 
@@ -144,6 +150,8 @@
     yield from scatter(7, two, part1, lambda part: part * sixteenth, last, ring2, store2)
     yield from gather(13, two, own, last)
     yield from gather(19, one, lambda part: place.core * half + part * quarter, sixteenth)
+    if not join:
+        return
     finals = []
     for part in range(2):
         mine = out.at[window(base + place.core * half + part * quarter, quarter)]
@@ -155,11 +163,13 @@
 
 def exchange_kernel(
     coefficients, order, bounds, phases, data_in, proj_in, targets_in, w_out, wh_out, feats_out, left_out,
-    data, proj, chosen, targets, feats, left, v, out, s1, slabs, *scratch
+    data, proj, chosen, targets, feats, left, v, out, s1, slabs, wh, parts, other, *scratch
 ):
     place = Place()
     buffers = scratch[:5 * len(CHUNKS)]
-    send_sem, recv_sem, plane_send, plane_recv, wide_send, wide_recv, load_sem, store_sem = scratch[5 * len(CHUNKS):]
+    send_sem, recv_sem, plane_send, plane_recv, wide_send, wide_recv, pair_send, pair_recv, load_sem, store_sem = (
+        scratch[5 * len(CHUNKS):]
+    )
     me, plane = place.row, place.plane
     height = data.shape[0]
     loads = [pltpu.make_async_copy(proj_in, proj, load_sem.at[0])]
@@ -230,7 +240,7 @@
             rhs = feats[turn_a, :, n * HALF:]
             put(GRAM + n * 2 * F, lax.dot_general(lhs, rhs, contract, preferred_element_type=F32))
 
-    G, C, M, N = range(4)
+    G, C, M0, M1, M2 = range(5)
     loads[0].wait()
     choose(turn_a)
     for t in range(TILES):
@@ -238,25 +248,29 @@
         features(turn_a, [t])
     gram()
     pl.semaphore_wait(barrier, len(greeted))
+    choose(turn_b)
+    features(turn_b, [0])
     advance(G)
-    choose(turn_b)
-    features(turn_b, range(3))
+    features(turn_b, [1])
+    features(turn_b, [2])
+    features(turn_b, [3])
     advance(G)
-    features(turn_b, range(3, TILES))
     loads[1 + TILES].wait()
     moments(0)
     choose(turn_c)
-    features(turn_c, range(2))
-    advance(M)
-    features(turn_c, range(2, TILES))
-    advance(G)
+    features(turn_c, [0])
+    advance(M0)
+    features(turn_c, [1])
+    features(turn_c, [2])
+    features(turn_c, [3])
     put(CROSS, lax.dot_general(feats[turn_a], feats[turn_x], contract, preferred_element_type=F32))
-    advance(C, M)
+    advance(C, M0)
     moments(1)
+    advance(M1, G, C, M0, G, M1, C, M0, G)
     moments(2)
     keep = pltpu.make_async_copy(feats.at[NBLK - 1], feats_out, store_sem.at[0])
     keep.start()
-    advance(G, C, N, M, N, G, C, M, N, G, C, M, N, C, G)
+    advance(M2, M1, C, M2, M0, G, M1, C, G)
 
     def wide(base, width, tall=F):
         return jnp.concatenate([out[window(base + k * tall, tall), :] for k in range(width // LANES)], axis=1)
@@ -282,23 +296,24 @@
     whole = jnp.concatenate([top, jnp.concatenate([top[:, HALF:].T, corner], axis=1)], axis=0)
     first = whole * scale + eye * (lower / center)
     s1[...] = first
-    row = lax.broadcasted_iota(jnp.int32, (SLAB, F), 0) + me * SLAB
-    column = lax.broadcasted_iota(jnp.int32, (SLAB, F), 1)
+    chip = lax.div(me, 2)
+    row = lax.broadcasted_iota(jnp.int32, (CHIP_SLAB, F), 0) + chip * CHIP_SLAB
+    column = lax.broadcasted_iota(jnp.int32, (CHIP_SLAB, F), 1)
     unit = (row == column).astype(F32)
-    value = k1 * (2.0 * unit - s1[window(me * SLAB, SLAB), :])
+    value = k1 * (2.0 * unit - s1[window(chip * CHIP_SLAB, CHIP_SLAB), :])
     part1 = split(first)
     second = k1 * (2.0 * first - dot3(part1, part1))
-    advance(M)
     part2 = split(second)
     value = k2 * (2.0 * value - dot3(split(value), part2))
     fourth = k2 * (2.0 * second - dot3(part2, part2))
-    advance(N)
     part4 = split(fourth)
     value = k4 * (2.0 * value - dot3(split(value), part4))
     once = dot3(split(value), part4)
     value = k8 * (2.0 * value - k4 * (2.0 * once - dot3(split(once), part4)))
     value = value * scale
-    sends = (plane != PLANES - 1, plane != 0)
+
+    inner = jnp.logical_and(plane != 0, plane != PLANES - 1)
+    edge = plane == 0
 
     def slab_copy(k, source, d):
         return pltpu.make_async_remote_copy(
@@ -307,10 +322,8 @@
             device_id={"cls": lax.rem(plane + d, PLANES)}, device_id_type=pl.DeviceIdType.MESH,
         )
 
-    def cross_planes(k, value):
-        slabs[plane, k] = value
-
-        @pl.when(sends[k])
+    def cross_planes(k, sends):
+        @pl.when(sends)
         def _():
             for d in (2, 1, 3):
                 slab_copy(k, plane, d).start()
@@ -320,12 +333,15 @@
         def _():
             slab_copy(k, source, 1).wait_recv()
 
-    cross_planes(0, value)
-    advance(M, C, C)
-    cross_planes(1, dot3(split(value), split(wide(CROSS, F))))
+    slabs[plane, 0] = value
+    cross_planes(0, edge)
+    advance(M2, M0, M1, C, M2, C)
+    slabs[plane, 1] = dot3(split(value), split(wide(CROSS, F)))
+    cross_planes(1, plane != 0)
+    cross_planes(0, inner)
 
     def moment(j):
-        return split(wide(MOMENT + 2 * F * j, 2 * LANES))
+        return split(out[window(MOMENT + 2 * F * j + place.core * F, F), :])
 
     def product(z, k, right):
         return dot3(split(slabs[z, k]), right)
@@ -334,63 +350,106 @@
         high, low = split(slabs[z, k])
         return jnp.dot(high, right, preferred_element_type=F32) + jnp.dot(low, right, preferred_element_type=F32)
 
-    def broadcast(j, w):
-        w_out[j] = w
-        mine = wh_out.at[j, pl.ds(pl.multiple_of(me * SLAB, SLAB), SLAB)]
-        wh_out[j, pl.ds(pl.multiple_of(me * SLAB, SLAB), SLAB), :] = w.astype(BF)
-
-        def tell(d, carry):
-            pltpu.make_async_remote_copy(
-                src_ref=mine, dst_ref=mine, send_sem=wide_send.at[j], recv_sem=wide_recv.at[j],
-                device_id={"rows": lax.rem(me + d, ROWS)}, device_id_type=pl.DeviceIdType.MESH,
-            ).start()
-            return carry
-
-        lax.fori_loop(1, ROWS, tell, 0)
-
-    def all_but_one(j):
-        part = wh_out.at[j, pl.ds(0, (ROWS - 1) * SLAB)]
+    def half(j):
+        return wh[j, place.core]
+
+    def pair_copy(n, ref):
         return pltpu.make_async_remote_copy(
-            src_ref=part, dst_ref=part, send_sem=wide_send.at[j], recv_sem=wide_recv.at[j],
+            src_ref=ref, dst_ref=ref, send_sem=pair_send.at[n], recv_sem=pair_recv.at[n],
             device_id=place.partner, device_id_type=pl.DeviceIdType.MESH,
         )
 
+    far_first = sorted(
+        ((dx, dy) for dx in range(4) for dy in range(4)),
+        key=lambda hop: -(min(hop[0], 4 - hop[0]) + min(hop[1], 4 - hop[1])),
+    )
+
+    def broadcast(j, w):
+        parts[place.core, j] = w[:SLAB]
+        other[j] = w[SLAB:]
+
+        @pl.when(place.core == 1)
+        def _():
+            parts[place.core, j] = w[SLAB:]
+            other[j] = w[:SLAB]
+
+        mine = wh.at[j, place.core, pl.ds(pl.multiple_of(chip * CHIP_SLAB, CHIP_SLAB), CHIP_SLAB)]
+        wh[j, place.core, pl.ds(pl.multiple_of(chip * CHIP_SLAB, CHIP_SLAB), CHIP_SLAB), :] = w.astype(BF)
+        for dx, dy in far_first:
+            there = (mod4(place.y + dy) * 4 + mod4(place.x + dx)) * 2
+            for swap in range(2 if j == NBLK - 1 else 1):
+                if dx == 0 and dy == 0 and swap == 0:
+                    continue
+                core = 1 - place.core if swap else place.core
+                pltpu.make_async_remote_copy(
+                    src_ref=mine, dst_ref=mine, send_sem=wide_send.at[j + swap], recv_sem=wide_recv.at[j + swap],
+                    device_id={"rows": there + core}, device_id_type=pl.DeviceIdType.MESH,
+                ).start()
+
+    def received(n):
+        j = min(n, NBLK - 1)
+        part = wh.at[j, 0, pl.ds(0, F if n == NBLK else F - CHIP_SLAB)]
+        return pltpu.make_async_remote_copy(
+            src_ref=part, dst_ref=part, send_sem=wide_send.at[n], recv_sem=wide_recv.at[n],
+            device_id=place.partner, device_id_type=pl.DeviceIdType.MESH,
+        )
+
+    def whole_half(j):
+        return jnp.concatenate([wh[j, 0], wh[j, 1]], axis=1)
+
     def subtract(turn, start):
+        both = whole_half(turn)
         for t in range(TILES):
             rows = pl.ds(t * TILE, TILE)
             before = targets[rows, :].astype(F32) if start else left[rows, :]
-            left[rows, :] = before - jnp.dot(feats[turn, rows, :], wh_out[turn], preferred_element_type=F32)
+            left[rows, :] = before - jnp.dot(feats[turn, rows, :], both, preferred_element_type=F32)
 
     arrived(0, 0)
     broadcast(0, product(0, 0, moment(0)))
-    advance(N, N)
-    assert all(done)
+    advance(M1, M2)
     arrived(0, 1)
     w1 = product(1, 0, moment(1))
-    arrived(0, 2)
-    w2 = product(2, 0, moment(2))
     for source in range(1, PLANES):
         arrived(1, source)
-    all_but_one(0).wait_recv()
-    broadcast(1, w1 - product2(1, 1, wh_out[0]))
-    w2 = w2 - product2(2, 1, wh_out[0])
+    received(0).wait_recv()
+    w1 = w1 - product2(1, 1, half(0))
+    broadcast(1, w1)
+    advance(M2)
+    assert all(done)
+    swaps = [pair_copy(0, wh.at[0, place.core])]
+    swaps[0].start()
+    arrived(0, 2)
+    w2 = product(2, 0, moment(2)) - product2(2, 1, half(0))
+    swaps[0].wait_recv()
     subtract(0, True)
-    all_but_one(1).wait_recv()
-    broadcast(2, w2 - product2(3, 1, wh_out[1]))
+    received(1).wait_recv()
+    broadcast(2, w2 - product2(3, 1, half(1)))
+    swaps.append(pair_copy(1, wh.at[1, place.core]))
+    swaps[1].start()
+    give = pltpu.make_async_remote_copy(
+        src_ref=other, dst_ref=parts.at[place.core], send_sem=pair_send.at[2], recv_sem=pair_recv.at[2],
+        device_id=place.partner, device_id_type=pl.DeviceIdType.MESH,
+    )
+    give.start()
+    swaps[1].wait_recv()
     subtract(1, False)
     hand = pltpu.make_async_copy(left, left_out, store_sem.at[1])
     hand.start()
-    all_but_one(2).wait_recv()
-    for copy in copies:
+    give.wait_recv()
+    w_out[...] = parts[...]
+    received(2).wait_recv()
+    received(NBLK).wait_recv()
+    wh_out[...] = whole_half(NBLK - 1)
+    for copy in copies + swaps + [give]:
         copy.wait_send()
-    for k in range(2):
-        @pl.when(sends[k])
+    for k, sends in ((0, plane != PLANES - 1), (1, plane != 0)):
+        @pl.when(sends)
         def _():
             for d in range(1, PLANES):
                 slab_copy(k, plane, d).wait_send()
 
-    for j in range(NBLK):
-        all_but_one(j).wait_send()
+    for n in range(NBLK + 1):
+        received(n).wait_send()
     keep.wait()
     hand.wait()
 
@@ -401,7 +460,7 @@
     hbm = pl.BlockSpec(memory_space=pl.ANY)
     rows, classes = targets.shape
     buffers = []
-    for _, height in CHUNKS:
+    for _, height, _ in CHUNKS:
         buffers += [
             pltpu.VMEM((height // 2, LANES), F32),
             pltpu.VMEM((height // 2, LANES), F32),
@@ -415,8 +474,8 @@
         in_specs=[smem, smem, vmem, hbm, hbm, hbm],
         out_specs=[vmem, vmem, hbm, hbm],
         out_shape=[
-            jax.ShapeDtypeStruct((NBLK, SLAB, classes), F32),
-            jax.ShapeDtypeStruct((NBLK, F, classes), BF),
+            jax.ShapeDtypeStruct((2, NBLK, SLAB, LANES), F32),
+            jax.ShapeDtypeStruct((F, classes), BF),
             jax.ShapeDtypeStruct((rows, F), BF),
             jax.ShapeDtypeStruct((rows, classes), F32),
         ],
@@ -430,12 +489,17 @@
             pltpu.VMEM((HEIGHT, LANES), F32),
             pltpu.VMEM((HEIGHT, LANES), F32),
             pltpu.VMEM((F, F), F32),
-            pltpu.VMEM((PLANES, 2, SLAB, F), F32),
+            pltpu.VMEM((PLANES, 2, CHIP_SLAB, F), F32),
+            pltpu.VMEM((NBLK, 2, F, LANES), BF),
+            pltpu.VMEM((2, NBLK, SLAB, LANES), F32),
+            pltpu.VMEM((NBLK, SLAB, LANES), F32),
             *buffers,
             dma((len(CHUNKS), COPIES)),
             dma((len(CHUNKS), COPIES)),
             dma((2, PLANES)),
             dma((2, PLANES)),
+            dma((NBLK + 1,)),
+            dma((NBLK + 1,)),
             dma((NBLK,)),
             dma((NBLK,)),
             dma((2 + TILES,)),
@@ -452,14 +516,14 @@
     def rows(t):
         return pl.ds(t * RESIDUAL_TILE, RESIDUAL_TILE)
 
-    loads = [pltpu.make_async_copy(half_in.at[NBLK - 1], half, load_sem.at[2 * tiles])]
+    loads = [pltpu.make_async_copy(half_in, half, load_sem.at[2 * tiles])]
     for t in range(tiles):
         loads.append(pltpu.make_async_copy(feats_in.at[rows(t)], feats.at[rows(t)], load_sem.at[2 * t]))
         loads.append(pltpu.make_async_copy(left_in.at[rows(t)], left.at[rows(t)], load_sem.at[2 * t + 1]))
     for copy in loads:
         copy.start()
     for turn in range(NBLK):
-        weights[order[turn]] = w[turn]
+        weights[order[turn]] = jnp.concatenate([w[0, turn], w[1, turn]], axis=1)
     loads[0].wait()
     stores = []
     for t in range(tiles):

time: 70.4 us -> 69.1 us (0.982)
  Pallas kernels: 69.4 us -> 68.1 us
    pallas_call x1, Pallas kernels: 64.1 us -> 62.8 us  [exchange_call(): pl.pallas_call(functools.partial(exchange_kernel, sine_coefficients(math....]
where the time goes in v6:
time: 69.1 us; the launch traced here: 68.9 us
  Pallas kernels  68.1 us (99%)
  between operations  0.8 us (1%)
    pallas_call x1, Pallas kernels, exchange_call(): pl.pallas_call(functools.partial(exchange_kernel, sine_coefficients(math....  62.8 us
    pallas_call x1, Pallas kernels, residual_call(): pl.pallas_call(residual_kernel, in_specs=[pl.BlockSpec(memory_space=pltpu...  5.31 us

profile of v6, /device:TPU:1, one launch (start us, length us, event | category | flops | bytes accessed | tf_op | source)
XLA Modules:
  0.0 68.9 jit_solution(12499563207704394141)
XLA Ops:
  0.6 62.8 %exchange.1 = (f32[2,3,16,128]{3,2,1,0:T(8,128)}, bf16[512,256]{1,0:T(8,128)(2,1)}, bf16[2048,512]{1,0:T(8,128)(2,1)}, f32[2048,256]{1,0:T(8,128)}) custom-call(s32[3]{0:T(128)} %order.3, f32[2,3]{1,0:T(2,128)} %bitcast.1, f32[1536]{0:T(1024)} %phases.1, bf16[2048,512]{1,0:T(8,128)(2,1)} %data_in.1, bf16[512,1536]{1,0:T(8,128)(2,1)} %proj_in.1, ...), custom_call_target="tpu_custom_call" | custom-call | tf_op jit(solution)/shard_map/exchange/pallas_call | solution.py:472
  63.5 5.3 %residual.1 = (f32[3,16,256]{2,1,0:T(8,128)}, f32[2048,256]{1,0:T(8,128)}) custom-call(s32[3]{0:T(128)} %order.3, f32[2,3,16,128]{3,2,1,0:T(8,128)} %get-tuple-element.6.w, bf16[2048,512]{1,0:T(8,128)(2,1)} %get-tuple-element.7.feats_in, bf16[512,256]{1,0:T(8,128)(2,1)} %get-tuple-element.8.half_in, f32[2048,256]{1,0:T(8,128)} %get-tuple-element.9.left_in), custom_call_target="tpu_custom_call" | custom-call | tf_op jit(solution)/shard_map/residual/pallas_call | solution.py:546

commit v7 on v6

--- a/solution.py
+++ b/solution.py
@@ -177,7 +177,7 @@
         rows = pl.ds(t * TILE, TILE)
         loads.append(pltpu.make_async_copy(data_in.at[rows], data.at[rows], load_sem.at[1 + t]))
     loads.append(pltpu.make_async_copy(targets_in, targets, load_sem.at[1 + TILES]))
-    for copy in loads:
+    for copy in loads[:3]:
         copy.start()
 
     barrier = pltpu.get_barrier_semaphore()
@@ -242,6 +242,8 @@
 
     G, C, M0, M1, M2 = range(5)
     loads[0].wait()
+    for copy in loads[3:]:
+        copy.start()
     choose(turn_a)
     for t in range(TILES):
         loads[1 + t].wait()
@@ -474,10 +476,10 @@
         in_specs=[smem, smem, vmem, hbm, hbm, hbm],
         out_specs=[vmem, vmem, hbm, hbm],
         out_shape=[
-            jax.ShapeDtypeStruct((2, NBLK, SLAB, LANES), F32),
-            jax.ShapeDtypeStruct((F, classes), BF),
-            jax.ShapeDtypeStruct((rows, F), BF),
-            jax.ShapeDtypeStruct((rows, classes), F32),
+            pltpu.VMEM((2, NBLK, SLAB, LANES), F32),
+            pltpu.VMEM((F, classes), BF),
+            pltpu.VMEM((rows, F), BF),
+            pltpu.VMEM((rows, classes), F32),
         ],
         scratch_shapes=[
             pltpu.VMEM(data.shape, BF),
@@ -505,33 +507,20 @@
             dma((2 + TILES,)),
             dma((2,)),
         ],
-        compiler_params=pltpu.CompilerParams(collective_id=0, has_side_effects=True),
+        compiler_params=pltpu.CompilerParams(collective_id=0, has_side_effects=True, vmem_limit_bytes=58500 << 10),
         name="exchange",
     )(order, bounds.T, phases, data, projections, targets)
 
 
-def residual_kernel(order, w, feats_in, half_in, left_in, weights, residual, feats, half, left, result, load_sem, store_sem):
-    tiles = left.shape[0] // RESIDUAL_TILE
-
-    def rows(t):
-        return pl.ds(t * RESIDUAL_TILE, RESIDUAL_TILE)
-
-    loads = [pltpu.make_async_copy(half_in, half, load_sem.at[2 * tiles])]
-    for t in range(tiles):
-        loads.append(pltpu.make_async_copy(feats_in.at[rows(t)], feats.at[rows(t)], load_sem.at[2 * t]))
-        loads.append(pltpu.make_async_copy(left_in.at[rows(t)], left.at[rows(t)], load_sem.at[2 * t + 1]))
-    for copy in loads:
-        copy.start()
+def residual_kernel(order, w, feats, half, left, weights, residual, result, store_sem):
     for turn in range(NBLK):
         weights[order[turn]] = jnp.concatenate([w[0, turn], w[1, turn]], axis=1)
-    loads[0].wait()
     stores = []
-    for t in range(tiles):
-        loads[1 + 2 * t].wait()
-        loads[2 + 2 * t].wait()
-        product = jnp.dot(feats[rows(t), :], half[...], preferred_element_type=F32)
-        result[rows(t), :] = left[rows(t), :] - product
-        copy = pltpu.make_async_copy(result.at[rows(t)], residual.at[rows(t)], store_sem.at[t])
+    for t in range(left.shape[0] // RESIDUAL_TILE):
+        rows = pl.ds(t * RESIDUAL_TILE, RESIDUAL_TILE)
+        product = jnp.dot(feats[rows, :], half[...], preferred_element_type=F32)
+        result[rows, :] = left[rows, :] - product
+        copy = pltpu.make_async_copy(result.at[rows], residual.at[rows], store_sem.at[t])
         copy.start()
         stores.append(copy)
     for copy in stores:
@@ -541,24 +530,19 @@
 def residual_call(order, feats, half, left, w):
     rows, classes = left.shape
     vmem = pl.BlockSpec(memory_space=pltpu.VMEM)
-    hbm = pl.BlockSpec(memory_space=pl.ANY)
-    tiles = rows // RESIDUAL_TILE
     return pl.pallas_call(
         residual_kernel,
-        in_specs=[pl.BlockSpec(memory_space=pltpu.SMEM), vmem, hbm, hbm, hbm],
-        out_specs=[vmem, hbm],
+        in_specs=[pl.BlockSpec(memory_space=pltpu.SMEM), vmem, vmem, vmem, vmem],
+        out_specs=[vmem, pl.BlockSpec(memory_space=pl.ANY)],
         out_shape=[
             jax.ShapeDtypeStruct((NBLK, SLAB, classes), F32),
             jax.ShapeDtypeStruct((rows, classes), F32),
         ],
         scratch_shapes=[
-            pltpu.VMEM((rows, F), BF),
-            pltpu.VMEM((F, classes), BF),
             pltpu.VMEM((rows, classes), F32),
-            pltpu.VMEM((rows, classes), F32),
-            pltpu.SemaphoreType.DMA((2 * tiles + 1,)),
-            pltpu.SemaphoreType.DMA((tiles,)),
+            pltpu.SemaphoreType.DMA((rows // RESIDUAL_TILE,)),
         ],
+        compiler_params=pltpu.CompilerParams(vmem_limit_bytes=24 << 20),
         name="residual",
     )(order, w, feats, half, left)
 

time: 69.1 us -> 66.2 us (0.958)
  Pallas kernels: 68.1 us -> 65.2 us
    pallas_call x1, Pallas kernels: 5.31 us -> 2.95 us  [residual_call(): pl.pallas_call(residual_kernel, in_specs=[pl.BlockSpec(memory_space=pltpu...]
where the time goes in v7:
time: 66.2 us; the launch traced here: 66 us
  Pallas kernels  65.2 us (98%)
  between operations  0.82 us (1%)
    pallas_call x1, Pallas kernels, exchange_call(): pl.pallas_call(functools.partial(exchange_kernel, sine_coefficients(math....  62.2 us
    pallas_call x1, Pallas kernels, residual_call(): pl.pallas_call(residual_kernel, in_specs=[pl.BlockSpec(memory_space=pltpu...  2.95 us

profile of v7, /device:TPU:1, one launch (start us, length us, event | category | flops | bytes accessed | tf_op | source)
XLA Modules:
  0.0 66.0 jit_solution(18363886354331929577)
XLA Ops:
  0.6 0.0 copy-start
  0.6 62.2 %exchange.1 = (f32[2,3,16,128]{3,2,1,0:T(8,128)S(1)}, bf16[512,256]{1,0:T(8,128)(2,1)S(1)}, bf16[2048,512]{1,0:T(8,128)(2,1)S(1)}, f32[2048,256]{1,0:T(8,128)S(1)}) custom-call(s32[3]{0:T(128)} %order.3, f32[2,3]{1,0:T(2,128)} %bitcast.1, f32[1536]{0:T(1024)} %phases.1, bf16[2048,512]{1,0:T(8,128)(2,1)} %data_in.1, bf16[512,1536]{1,0:T(8,128)(2,1)} %proj_in.1, ...), custom_call_target="tpu_custom_call" | custom-call | tf_op jit(solution)/shard_map/exchange/pallas_call | solution.py:474
  62.9 0.0 copy-done
  62.9 3.0 %residual.1 = (f32[3,16,256]{2,1,0:T(8,128)}, f32[2048,256]{1,0:T(8,128)}) custom-call(s32[3]{0:T(128)S(1)} %copy-done, f32[2,3,16,128]{3,2,1,0:T(8,128)S(1)} %get-tuple-element.6.w, bf16[2048,512]{1,0:T(8,128)(2,1)S(1)} %get-tuple-element.7.feats, bf16[512,256]{1,0:T(8,128)(2,1)S(1)} %get-tuple-element.8.half, f32[2048,256]{1,0:T(8,128)S(1)} %get-tuple-element.9.left), custom_call_target="tpu_custom_call" | custom-call | tf_op jit(solution)/shard_map/residual/pallas_call | solution.py:533
Async XLA Ops:
  0.6 62.2 %copy-start = (s32[3]{0:T(128)S(1)}, s32[3]{0:T(128)}, u32[]{:S(2)}) copy-start(s32[3]{0:T(128)} %order.3) | copy-start | bytes 40

commit v8 on v7

--- a/solution.py
+++ b/solution.py
@@ -11,7 +11,7 @@
 F = 512
 NBLK = 3
 TILE = 512
-RESIDUAL_TILE = 512
+RESIDUAL_TILE = 1024
 TILES = 4
 SLAB = 16
 BF = jnp.bfloat16

time: 66.2 us -> 66.4 us (level)
  no operation moved by 1% of the time
where the time goes in v8:
time: 66.4 us; the launch traced here: 66.3 us
  Pallas kernels  65.5 us (99%)
  between operations  0.82 us (1%)
    pallas_call x1, Pallas kernels, exchange_call(): pl.pallas_call(functools.partial(exchange_kernel, sine_coefficients(math....  62.2 us
    pallas_call x1, Pallas kernels, residual_call(): pl.pallas_call(residual_kernel, in_specs=[pl.BlockSpec(memory_space=pltpu...  3.22 us

profile of v8, /device:TPU:1, one launch (start us, length us, event | category | flops | bytes accessed | tf_op | source)
XLA Modules:
  0.0 66.3 jit_solution(1453763423618431581)
XLA Ops:
  0.6 0.0 copy-start
  0.6 62.2 %exchange.1 = (f32[2,3,16,128]{3,2,1,0:T(8,128)S(1)}, bf16[512,256]{1,0:T(8,128)(2,1)S(1)}, bf16[2048,512]{1,0:T(8,128)(2,1)S(1)}, f32[2048,256]{1,0:T(8,128)S(1)}) custom-call(s32[3]{0:T(128)} %order.3, f32[2,3]{1,0:T(2,128)} %bitcast.1, f32[1536]{0:T(1024)} %phases.1, bf16[2048,512]{1,0:T(8,128)(2,1)} %data_in.1, bf16[512,1536]{1,0:T(8,128)(2,1)} %proj_in.1, ...), custom_call_target="tpu_custom_call" | custom-call | tf_op jit(solution)/shard_map/exchange/pallas_call | solution.py:474
  62.9 0.0 copy-done
  62.9 3.2 %residual.1 = (f32[3,16,256]{2,1,0:T(8,128)}, f32[2048,256]{1,0:T(8,128)}) custom-call(s32[3]{0:T(128)S(1)} %copy-done, f32[2,3,16,128]{3,2,1,0:T(8,128)S(1)} %get-tuple-element.6.w, bf16[2048,512]{1,0:T(8,128)(2,1)S(1)} %get-tuple-element.7.feats, bf16[512,256]{1,0:T(8,128)(2,1)S(1)} %get-tuple-element.8.half, f32[2048,256]{1,0:T(8,128)S(1)} %get-tuple-element.9.left), custom_call_target="tpu_custom_call" | custom-call | tf_op jit(solution)/shard_map/residual/pallas_call | solution.py:533
Async XLA Ops:
  0.6 62.2 %copy-start = (s32[3]{0:T(128)S(1)}, s32[3]{0:T(128)}, u32[]{:S(2)}) copy-start(s32[3]{0:T(128)} %order.3) | copy-start | bytes 40
